TPU v7x, 512 devices: a whole 4x4x16 slice. The times are simulated.
512 devices in a mesh: dp: 16 (over x_lo, y, core), vocab: 32 (over z, x_hi).
Axes of the slice: x: 4 (x_hi: 2, x_lo: 2; x = x_hi * 2 + x_lo), y: 4, z: 16, core: 2. Of those that a mesh axis runs over, the one named last changes fastest.
Arguments:
- passage_hidden: bfloat16 [2048, 2048], P('dp'), may hold values from -7 to 7
- passage_lengths: int32 [32], P('dp'), may hold values from 16 to 64, as said below
- query_ids: int32 [32, 16], P('dp'), may hold values from 0 to 131071
- query_lengths: int32 [32], P('dp'), may hold values from 4 to 16, as said below
- positives: int32 [32], replicated, may hold values from 0 to 31, each once
- head: bfloat16 [2048, 131072], P('dp', 'vocab'), may hold values from -0.125 to 0.125
- df_prev: float32 [131072], P('vocab'), may hold values from 1 to 4096
Outputs:
- head_grad: float32 [2048, 131072], P('dp', 'vocab')
- scores: float32 [32, 32], replicated
Inputs may be any that keep to these rules, and one draw needn't show every extreme that they name: `passage_lengths`: some passage fills all 64 slots. `query_lengths`: some query fills all 16 slots. `positives`: each passage is the positive of exactly one query.
All inputs are finite; a program needn't handle non-finite values.
Results may differ from a plain program's by a relative error of at most 0.00064.
Values may be sent and summed in bfloat16 or wider, within the bound.
No kernel may reach another device: no remote copies, remote signals or barrier semaphores. Data moves between devices by JAX's collectives and lax.ppermute only.
A program may use at most 64 MiB of HBM per device.

v0:
```python
import jax
import jax.numpy as jnp
from jax import lax
from jax.sharding import PartitionSpec as P

flops_weight = 0.3


def ranking_grad(scores, chosen, query_total):
    columns = scores.shape[1]
    onehot = (jnp.arange(columns, dtype=jnp.int32)[None, :] == chosen[:, None]).astype(jnp.float32)
    own_score = jnp.sum(scores * onehot, axis=1, keepdims=True)
    sigmas = jax.nn.sigmoid(scores - own_score)
    return (sigmas - onehot * jnp.sum(sigmas, axis=1, keepdims=True)) / query_total


def local(passage_hidden, passage_lengths, query_ids, query_lengths, positives, head, df_prev):
    dp_count = lax.axis_size("dp")
    dp_index = lax.axis_index("dp")
    vocab_index = lax.axis_index("vocab")
    width_local = head.shape[1]
    column_count = width_local // dp_count
    head_block = lax.all_to_all(head, "dp", split_axis=1, concat_axis=0, tiled=True)
    hidden_all, passage_sizes, query_tokens, query_sizes = (
        lax.all_gather(passage_hidden, "dp", axis=0, tiled=True),
        lax.all_gather(passage_lengths, "dp", axis=0, tiled=True),
        lax.all_gather(query_ids, "dp", axis=0, tiled=True),
        lax.all_gather(query_lengths, "dp", axis=0, tiled=True),
    )
    passage_count = passage_sizes.shape[0]
    seq_span = hidden_all.shape[0] // passage_count
    logits = jnp.dot(hidden_all, head_block, preferred_element_type=jnp.float32)
    softened = jax.nn.softplus(logits)
    activation = jnp.log1p(softened)
    slope_term = jax.nn.sigmoid(logits) / (1.0 + softened)
    positions = jnp.arange(seq_span, dtype=jnp.int32)
    token_mask = (positions[None, :] < passage_sizes[:, None]).astype(jnp.float32)
    token_weight = token_mask / passage_sizes.astype(jnp.float32)[:, None]
    passage_rep = jnp.sum(
        activation.reshape(passage_count, seq_span, column_count) * token_weight[:, :, None], axis=1
    )
    first_column = dp_index * column_count
    doc_freq = lax.dynamic_slice_in_dim(df_prev, first_column, column_count, 0) + jnp.sum(
        1.0 - jnp.exp(-2.0 * passage_rep), axis=0
    )
    term_weight = jnp.log1p(doc_freq)
    column_ids = (
        vocab_index * width_local + first_column + jnp.arange(column_count, dtype=jnp.int32)
    )
    query_mask = jnp.arange(query_tokens.shape[1], dtype=jnp.int32)[None, :] < query_sizes[:, None]
    matches = (query_tokens[:, :, None] == column_ids[None, None, :]) & query_mask[:, :, None]
    query_bag = jnp.sum(matches.astype(jnp.float32), axis=1)
    partial_scores = jnp.dot(
        query_bag,
        passage_rep.T,
        precision=lax.Precision.HIGHEST,
        preferred_element_type=jnp.float32,
    )
    query_total = positives.shape[0]
    scores = lax.psum(partial_scores, ("dp", "vocab"))
    score_grad = ranking_grad(scores, positives, query_total)
    rep_grad = jnp.dot(
        score_grad.T, query_bag, precision=lax.Precision.HIGHEST, preferred_element_type=jnp.float32
    )
    rep_grad = rep_grad + 2.0 * flops_weight / passage_count * term_weight * jnp.mean(
        passage_rep, axis=0
    )
    logit_grad = (
        (token_weight[:, :, None] * rep_grad[:, None, :]).reshape(logits.shape) * slope_term
    ).astype(jnp.bfloat16)
    grad_block = lax.dot_general(
        hidden_all, logit_grad, (((0,), (0,)), ((), ())), preferred_element_type=jnp.float32
    )
    head_grad = lax.all_to_all(grad_block, "dp", split_axis=0, concat_axis=1, tiled=True)
    return (head_grad, scores)


def solution(mesh):
    return jax.shard_map(
        local,
        mesh=mesh,
        in_specs=(
            P("dp", None),
            P("dp"),
            P("dp", None),
            P("dp"),
            P(),
            P("dp", "vocab"),
            P("vocab"),
        ),
        out_specs=(P("dp", "vocab"), P()),
        check_vma=False,
    )
```

profile of v0, /device:TPU:1, one launch (start us, length us, event | category | flops | bytes accessed | tf_op | source)
XLA Modules:
  0.0 239.4 jit_solution(17797994850727579767)
XLA Ops:
  7.2 0.0 all-gather.3.cloned.1.call-start
  7.2 0.7 all-gather.3.cloned.1.call-update
  7.9 0.0 copy-start.3
  7.9 0.0 copy-start.4
  7.9 0.0 copy-start.1
  7.9 2.3 copy.18
  10.2 10.3 %all-to-all-start = ((bf16[128,16,256]{0,2,1:T(8,128)(2,1)}), bf16[128,16,256]{0,2,1:T(8,128)(2,1)S(1)}, u32[]{:S(2)}, u32[]{:S(2)}) async-start(bf16[128,16,256]{0,2,1:T(8,128)(2,1)} %bitcast.3), calls=%async_computation | async-start | bytes 2097152 | tf_op jit(solution)/shard_map/all_to_all | solution.py:23
  20.5 1.3 dynamic-slice
  22.4 0.0 copy-done.3
  22.4 0.2 dynamic-update-slice
  22.7 0.0 copy-done.4
  22.7 0.2 dynamic-update-slice.1
  22.9 18.3 %all-reduce.2 = (s32[32]{0:T(128)S(1)}, s32[32]{0:T(128)S(1)}) all-reduce(s32[32]{0:T(128)S(1)} %dynamic-update-slice.1, s32[32]{0:T(128)S(1)} %dynamic-update-slice), channel_id=1, replica_groups=mesh['dp'=16,'vocab'=32] {'dp'}, use_global_device_ids=true, to_apply=%add.1 | all-reduce | flops 64 | bytes 512
  41.2 0.1 convert_divide_fusion
  41.3 0.1 div.37
  41.4 0.0 copy-done.1
  41.4 19.2 %all-gather = s32[16,2,16]{2,1,0:T(2,128)S(1)} all-gather(s32[1,2,16]{2,1,0:T(2,128)S(1)} %bitcast.35), channel_id=1, replica_groups=mesh['dp'=16,'vocab'=32] {'dp'}, dimensions={0}, use_global_device_ids=true | all-gather | bytes 2176 | tf_op jit(solution)/shard_map/all_gather | solution.py:27
  60.6 0.1 iota_compare_fusion.2
  60.7 0.3 convert_reduce_fusion
  60.9 0.0 all-to-all-done
  61.0 0.5 copy.19
  61.5 15.2 %all-gather.3.cloned.1.call-done = bf16[2048,2048]{1,0:T(8,128)(2,1)} async-done(((bf16[128,2048]{1,0:T(8,128)(2,1)}), bf16[2048,2048]{1,0:T(8,128)(2,1)}) %all-gather.3.cloned.1.call-update) | async-done | bytes 8388624 | tf_op jit(solution)/shard_map/all_gather | solution.py:25
  76.7 7.4 %multiply_reduce_fusion = (f32[256]{0:T(256)S(1)}, f32[2048,256]{1,0:T(8,128)S(1)}) fusion(f32[2048]{0:T(1024)S(1)} %div.37, bf16[2048,2048]{1,0:T(8,128)(2,1)} %all-gather.3.cloned.1.call-done, bf16[2048,256]{1,0:T(8,128)(2,1)S(1)} %bitcast.33), kind=kOutput, calls=%fused_computation.5 | convolution fusion | flops 2151677696 | bytes 11543552 | tf_op jit(solution)/shard_map/dot_general | solution.py:32
  84.1 0.0 copy-start.2
  84.1 1.9 multiply_reduce_fusion.1
  86.1 0.2 fusion.13
  86.2 105.4 %psum.7 = f32[32,32]{1,0:T(8,128)S(1)} all-reduce(f32[32,32]{1,0:T(8,128)S(1)} %fusion.13), channel_id=1, replica_groups=mesh['dp'=16,'vocab'=32] {'dp','vocab'}, use_global_device_ids=true, to_apply=%region_2.3 | all-reduce | flops 1024 | bytes 8192 | tf_op jit(solution)/shard_map/psum | solution.py:60
  191.6 0.0 copy-done.2
  191.6 0.0 copy-start
  191.6 0.2 select_reduce_fusion
  191.8 0.2 fusion.12
  192.0 0.8 multiply_multiply_fusion
  192.8 0.3 convolution_add_fusion
  193.1 1.7 fusion.1
  194.9 5.7 %convolution_bitcast_fusion = f32[32,16,8,128]{3,2,1,0:T(8,128)S(1)} fusion(bf16[2048,256]{1,0:T(8,128)(2,1)S(1)} %fusion.1, bf16[2048,2048]{1,0:T(8,128)(2,1)} %all-gather.3.cloned.1.call-done), kind=kOutput, calls=%fused_computation.8 | convolution fusion | flops 2147483648 | bytes 11534336 | tf_op jit(solution)/shard_map/dot_general | solution.py:71
  200.6 0.0 copy-done
  200.6 0.2 copy.24
  200.8 30.0 %all_to_all.38 = f32[16,128,256]{1,2,0:T(8,128)S(1)} all-to-all(f32[16,128,256]{1,2,0:T(8,128)S(1)} %bitcast.30), channel_id=1, replica_groups=mesh['dp'=16,'vocab'=32] {'dp'}, dimensions={0} | all-to-all | bytes 4194304 | tf_op jit(solution)/shard_map/all_to_all | solution.py:74
  230.8 1.8 copy.21
  (5 shorter events, 0.0 us)
Async XLA Ops:
  7.2 69.5 %all-gather.3.cloned.1.call-start = ((), (), s32[]{:S(2)}) async-start(), calls=%async_computation.2 | async-start | bytes 8912896 | tf_op jit(solution)/shard_map/all_gather | solution.py:25
  7.9 14.5 %copy-start.3 = (s32[2]{0:T(128)S(1)}, s32[2]{0:T(128)}, u32[]{:S(2)}) copy-start(s32[2]{0:T(128)} %param.8) | copy-start | bytes 28
  7.9 14.8 %copy-start.4 = (s32[2]{0:T(128)S(1)}, s32[2]{0:T(128)}, u32[]{:S(2)}) copy-start(s32[2]{0:T(128)} %param.10) | copy-start | bytes 28
  7.9 33.5 %copy-start.1 = (s32[2,16]{1,0:T(2,128)S(1)}, s32[2,16]{1,0:T(2,128)}, u32[]{:S(2)}) copy-start(s32[2,16]{1,0:T(2,128)} %param.9) | copy-start | bytes 388
  10.2 50.7 %all-to-all-start = ((bf16[128,16,256]{0,2,1:T(8,128)(2,1)}), bf16[128,16,256]{0,2,1:T(8,128)(2,1)S(1)}, u32[]{:S(2)}, u32[]{:S(2)}) async-start(bf16[128,16,256]{0,2,1:T(8,128)(2,1)} %bitcast.3), calls=%async_computation | async-start | bytes 2097152 | tf_op jit(solution)/shard_map/all_to_all | solution.py:23
  84.1 107.6 %copy-start.2 = (s32[32]{0:T(128)S(1)}, s32[32]{0:T(128)}, u32[]{:S(2)}) copy-start(s32[32]{0:T(128)} %param.11) | copy-start | bytes 388
  191.6 9.0 %copy-start = (f32[32,32]{1,0:T(8,128)}, f32[32,32]{1,0:T(8,128)S(1)}, u32[]{:S(2)}) copy-start(f32[32,32]{1,0:T(8,128)S(1)} %psum.7) | copy-start | bytes 12292
Sparse Core Ops, SparseCore 0:
  10.1 66.5 all-gather.2
where the time goes:
time: 240 us; the launch traced here: 239 us
  blocking collectives  173 us (72%)
  waiting for transfers between devices  15.9 us (7%)
  between operations  14.8 us (6%)
  matrix products  13.6 us (6%)
  starting transfers between devices  10.3 us (4%)
  local copies, waits for them, and re-layouts  6.64 us (3%)
  other arithmetic  5.26 us (2%)
    psum x1, blocking collectives, local(): scores = lax.psum(partial_scores, ('dp', 'vocab'))  105 us
    all_to_all x1, blocking collectives, local(): lax.all_to_all(grad_block, 'dp', split_axis=0, concat_axis=1, tiled=True)  30 us
    all_gather x1, blocking collectives, local(): lax.all_gather(query_ids, 'dp', axis=0, tiled=True)  19.2 us
    unnamed x1, blocking collectives  18.3 us
    all_gather x1, waiting for transfers between devices, local(): lax.all_gather(passage_hidden, 'dp', axis=0, tiled=True)  15.2 us
    all_to_all x1, starting transfers between devices, local(): lax.all_to_all(head, 'dp', split_axis=1, concat_axis=0, tiled=True)  10.3 us
    dot_general x1, matrix products, local(): logits = jnp.dot(hidden_all, head_block, preferred_element_type=jnp.float32)  7.39 us
    unnamed x17, local copies, waits for them, and re-layouts  5.83 us
  transfers between devices with their start and end apart: 2, of which 1 were waited for; matrix products, arithmetic and copies ran while one was open for 2% of the time, Pallas kernels for 0%

commit v1 on v0

--- a/solution.py
+++ b/solution.py
@@ -1,9 +1,12 @@
 import jax
 import jax.numpy as jnp
 from jax import lax
-from jax.sharding import PartitionSpec as P
+from jax.sharding import Mesh, PartitionSpec as P
 
 flops_weight = 0.3
+DP = ("xl", "y", "c")
+VOCAB = ("z", "xh")
+PLANE = ("xl", "y", "c", "xh")
 
 
 def ranking_grad(scores, chosen, query_total):
@@ -14,19 +17,27 @@
     return (sigmas - onehot * jnp.sum(sigmas, axis=1, keepdims=True)) / query_total
 
 
+def spread(value, axes):
+    count = lax.axis_size(axes)
+    return lax.all_to_all(
+        jnp.broadcast_to(value[None], (count,) + value.shape), axes, 0, 0, tiled=True
+    )
+
+
 def local(passage_hidden, passage_lengths, query_ids, query_lengths, positives, head, df_prev):
-    dp_count = lax.axis_size("dp")
-    dp_index = lax.axis_index("dp")
-    vocab_index = lax.axis_index("vocab")
+    dp_count = lax.axis_size(DP)
+    dp_index = lax.axis_index(DP)
+    vocab_index = lax.axis_index(VOCAB)
     width_local = head.shape[1]
     column_count = width_local // dp_count
-    head_block = lax.all_to_all(head, "dp", split_axis=1, concat_axis=0, tiled=True)
-    hidden_all, passage_sizes, query_tokens, query_sizes = (
-        lax.all_gather(passage_hidden, "dp", axis=0, tiled=True),
-        lax.all_gather(passage_lengths, "dp", axis=0, tiled=True),
-        lax.all_gather(query_ids, "dp", axis=0, tiled=True),
-        lax.all_gather(query_lengths, "dp", axis=0, tiled=True),
-    )
+    query_slots = query_ids.shape[1]
+    packed = jnp.concatenate([query_ids, query_lengths[:, None], passage_lengths[:, None]], axis=1)
+    packed = spread(packed, DP).reshape(-1, query_slots + 2)
+    query_tokens = packed[:, :query_slots]
+    query_sizes = packed[:, query_slots]
+    passage_sizes = packed[:, query_slots + 1]
+    head_block = lax.all_to_all(head, DP, split_axis=1, concat_axis=0, tiled=True)
+    hidden_all = lax.all_gather(passage_hidden, DP, axis=0, tiled=True)
     passage_count = passage_sizes.shape[0]
     seq_span = hidden_all.shape[0] // passage_count
     logits = jnp.dot(hidden_all, head_block, preferred_element_type=jnp.float32)
@@ -47,7 +58,7 @@
     column_ids = (
         vocab_index * width_local + first_column + jnp.arange(column_count, dtype=jnp.int32)
     )
-    query_mask = jnp.arange(query_tokens.shape[1], dtype=jnp.int32)[None, :] < query_sizes[:, None]
+    query_mask = jnp.arange(query_slots, dtype=jnp.int32)[None, :] < query_sizes[:, None]
     matches = (query_tokens[:, :, None] == column_ids[None, None, :]) & query_mask[:, :, None]
     query_bag = jnp.sum(matches.astype(jnp.float32), axis=1)
     partial_scores = jnp.dot(
@@ -57,7 +68,8 @@
         preferred_element_type=jnp.float32,
     )
     query_total = positives.shape[0]
-    scores = lax.psum(partial_scores, ("dp", "vocab"))
+    plane_scores = jnp.sum(spread(partial_scores, PLANE), axis=0)
+    scores = jnp.sum(spread(plane_scores, "z"), axis=0)
     score_grad = ranking_grad(scores, positives, query_total)
     rep_grad = jnp.dot(
         score_grad.T, query_bag, precision=lax.Precision.HIGHEST, preferred_element_type=jnp.float32
@@ -71,23 +83,24 @@
     grad_block = lax.dot_general(
         hidden_all, logit_grad, (((0,), (0,)), ((), ())), preferred_element_type=jnp.float32
     )
-    head_grad = lax.all_to_all(grad_block, "dp", split_axis=0, concat_axis=1, tiled=True)
+    head_grad = lax.all_to_all(grad_block, DP, split_axis=0, concat_axis=1, tiled=True)
     return (head_grad, scores)
 
 
 def solution(mesh):
+    fine = Mesh(mesh.devices.reshape(2, 4, 2, 16, 2), DP + VOCAB)
     return jax.shard_map(
         local,
-        mesh=mesh,
+        mesh=fine,
         in_specs=(
-            P("dp", None),
-            P("dp"),
-            P("dp", None),
-            P("dp"),
+            P(DP, None),
+            P(DP),
+            P(DP, None),
+            P(DP),
             P(),
-            P("dp", "vocab"),
-            P("vocab"),
+            P(DP, VOCAB),
+            P(VOCAB),
         ),
-        out_specs=(P("dp", "vocab"), P()),
+        out_specs=(P(DP, VOCAB), P()),
         check_vma=False,
     )

time: 240 us -> 186 us (0.78)
  blocking collectives: 173 us -> 31.3 us
  waiting for transfers between devices: 15.9 us -> 76.5 us
  starting transfers between devices: 10.3 us -> 32.3 us
  local copies, waits for them, and re-layouts: 6.64 us -> 9.72 us
  other arithmetic: 5.26 us -> 8.02 us
    psum x1 -> x0, blocking collectives: 105 us -> none  [local(): scores = lax.psum(partial_scores, ('dp', 'vocab'))]
    all_to_all x1 -> x4, waiting for transfers between devices: 0.01 us -> 46.5 us  [the longest x1 24.5 us: local(): lax.all_to_all(head, DP, split_axis=1, concat_axis=0, tiled=True)]
    all_to_all x1 -> x4, starting transfers between devices: 10.3 us -> 32.3 us  [the longest x3 28.4 us: spread(): lax.all_to_all(jnp.broadcast_to(value[None], (count,) + value.shape), axe...]
    all_gather x1 -> x0, blocking collectives: 19.2 us -> none  [local(): lax.all_gather(query_ids, 'dp', axis=0, tiled=True)]
    unnamed x1 -> x0, blocking collectives: 18.3 us -> none
    all_gather x1, waiting for transfers between devices: 15.2 us -> 29.3 us  [local(): hidden_all = lax.all_gather(passage_hidden, DP, axis=0, tiled=True)]
    unnamed x17 -> x10, local copies, waits for them, and re-layouts: 5.83 us -> 6.06 us
  transfers between devices with their start and end apart: 2 -> 5, of which waited for: 1 -> 5; matrix products, arithmetic and copies ran while one was open for 2% -> 4% of each run, Pallas kernels for 0% -> 0%
where the time goes in v1:
time: 186 us
  waiting for transfers between devices  76.5 us (41%)
  starting transfers between devices  32.3 us (17%)
  blocking collectives  31.3 us (17%)
  between operations  14.2 us (8%)
  matrix products  13.6 us (7%)
  local copies, waits for them, and re-layouts  9.72 us (5%)
  other arithmetic  8.02 us (4%)
    all_to_all x1, blocking collectives, local(): lax.all_to_all(grad_block, DP, split_axis=0, concat_axis=1, tiled=True)  31.3 us
    all_gather x1, waiting for transfers between devices, local(): hidden_all = lax.all_gather(passage_hidden, DP, axis=0, tiled=True)  29.3 us
    all_to_all x3, starting transfers between devices, spread(): lax.all_to_all(jnp.broadcast_to(value[None], (count,) + value.shape), axe...  28.4 us
    all_to_all x1, waiting for transfers between devices, local(): lax.all_to_all(head, DP, split_axis=1, concat_axis=0, tiled=True)  24.5 us
    all_to_all x3, waiting for transfers between devices, spread(): lax.all_to_all(jnp.broadcast_to(value[None], (count,) + value.shape), axe...  22 us
    dot_general x1, matrix products, local(): logits = jnp.dot(hidden_all, head_block, preferred_element_type=jnp.float32)  7.39 us
    unnamed x10, local copies, waits for them, and re-layouts  6.06 us
    dot_general x1, matrix products, local(): lax.dot_general(hidden_all, logit_grad, (((0,), (0,)), ((), ())), preferr...  5.74 us
  transfers between devices with their start and end apart: 5, of which 5 were waited for; matrix products, arithmetic and copies ran while one was open for 4% of the time, Pallas kernels for 0%

profile of v1, /device:TPU:1, one launch (start us, length us, event | category | flops | bytes accessed | tf_op | source)
XLA Modules:
  0.0 185.7 jit_solution(16136462028311963725)
XLA Ops:
  7.2 0.0 all-gather.2.cloned.1.call-start
  7.2 0.7 all-gather.2.cloned.1.call-update
  7.9 0.7 copy.29
  8.6 0.7 copy.28
  9.4 0.8 pad_add_fusion
  10.1 0.6 broadcast_in_dim.12
  10.7 10.1 %all-to-all-start = ((s32[16,2,18]{2,1,0:T(2,128)}), s32[16,2,18]{2,1,0:T(2,128)S(1)}, u32[]{:S(2)}, u32[]{:S(2)}) async-start(s32[16,2,18]{2,1,0:T(2,128)} %broadcast_in_dim.12), calls=%async_computation | async-start | bytes 32768 | tf_op jit(solution)/shard_map/all_to_all | solution.py:22
  20.9 2.3 %copy.30 = bf16[128,4096]{0,1:T(8,128)(2,1)} copy(bf16[128,4096]{1,0:T(8,128)(2,1)} %param.12) | data formatting | bytes 2097152 | tf_op args[5]
  23.1 3.6 %all-to-all-done = s32[16,2,18]{2,1,0:T(2,128)S(1)} async-done(((s32[16,2,18]{2,1,0:T(2,128)}), s32[16,2,18]{2,1,0:T(2,128)S(1)}, u32[]{:S(2)}, u32[]{:S(2)}) %all-to-all-start) | async-done | bytes 2336 | tf_op jit(solution)/shard_map/all_to_all | solution.py:22
  26.7 3.8 %all-to-all-start.1 = ((bf16[128,16,256]{0,2,1:T(8,128)(2,1)}), bf16[128,16,256]{0,2,1:T(8,128)(2,1)S(1)}, u32[]{:S(2)}, u32[]{:S(2)}) async-start(bf16[128,16,256]{0,2,1:T(8,128)(2,1)} %bitcast.3), calls=%async_computation.1 | async-start | bytes 2097152 | tf_op jit(solution)/shard_map/all_to_all | solution.py:39
  30.6 0.2 convert_reduce_fusion.1
  30.8 0.2 slice_reduce_fusion.1
  30.9 0.1 convert_divide_fusion
  31.0 0.1 div.40
  31.1 0.1 iota_compare_fusion.2
  31.2 0.3 convert_reduce_fusion
  31.4 24.5 %all-to-all-done.1 = bf16[128,16,256]{0,2,1:T(8,128)(2,1)S(1)} async-done(((bf16[128,16,256]{0,2,1:T(8,128)(2,1)}), bf16[128,16,256]{0,2,1:T(8,128)(2,1)S(1)}, u32[]{:S(2)}, u32[]{:S(2)}) %all-to-all-start.1) | async-done | bytes 1048608 | tf_op jit(solution)/shard_map/all_to_all | solution.py:39
  55.9 0.5 copy.31
  56.5 29.3 %all-gather.2.cloned.1.call-done = bf16[2048,2048]{1,0:T(8,128)(2,1)} async-done(((bf16[128,2048]{1,0:T(8,128)(2,1)}), bf16[2048,2048]{1,0:T(8,128)(2,1)}) %all-gather.2.cloned.1.call-update) | async-done | bytes 8388624 | tf_op jit(solution)/shard_map/all_gather | solution.py:40
  85.7 7.4 %multiply_reduce_fusion = (f32[256]{0:T(256)S(1)}, f32[2048,256]{1,0:T(8,128)S(1)}) fusion(f32[2048]{0:T(1024)S(1)} %div.40, bf16[2048,2048]{1,0:T(8,128)(2,1)} %all-gather.2.cloned.1.call-done, bf16[2048,256]{1,0:T(8,128)(2,1)S(1)} %bitcast.34), kind=kOutput, calls=%fused_computation.5 | convolution fusion | flops 2151677696 | bytes 11543552 | tf_op jit(solution)/shard_map/dot_general | solution.py:43
  93.1 1.9 %multiply_reduce_fusion.1 = f32[32,256]{1,0:T(8,128)S(1)} fusion(f32[32,64]{1,0:T(8,128)S(1)} %convert_divide_fusion, f32[2048,256]{1,0:T(8,128)S(1)} %get-tuple-element.9), kind=kLoop, calls=%fused_computation.6 | loop fusion | flops 4186112 | bytes 2138112 | tf_op jit(solution)/shard_map/reduce_sum | solution.py:50
  95.1 0.2 fusion.13
  95.2 0.0 copy-start.1
  95.2 0.1 broadcast_in_dim.13
  95.3 0.9 reshape.108
  96.2 5.2 %all-to-all-start.2 = ((f32[32,1,1024]{2,1,0:T(1,128)}), f32[32,1,1024]{2,1,0:T(1,128)S(1)}, u32[]{:S(2)}, u32[]{:S(2)}) async-start(f32[32,1,1024]{2,1,0:T(1,128)} %reshape.108), calls=%async_computation.2 | async-start | bytes 262144 | tf_op jit(solution)/shard_map/all_to_all | solution.py:22
  101.4 7.7 %all-to-all-done.2 = f32[32,1,1024]{2,1,0:T(1,128)S(1)} async-done(((f32[32,1,1024]{2,1,0:T(1,128)}), f32[32,1,1024]{2,1,0:T(1,128)S(1)}, u32[]{:S(2)}, u32[]{:S(2)}) %all-to-all-start.2) | async-done | bytes 131104 | tf_op jit(solution)/shard_map/all_to_all | solution.py:22
  109.1 0.5 broadcast.88
  109.6 0.9 reduce.8
  110.6 0.2 reshape.109
  110.8 0.1 reduce_sum.74
  110.8 0.8 reshape.110
  111.6 13.1 %all-to-all-start.3 = ((f32[16,1,1024]{2,1,0:T(1,128)}), f32[16,1,1024]{2,1,0:T(1,128)S(1)}, u32[]{:S(2)}, u32[]{:S(2)}) async-start(f32[16,1,1024]{2,1,0:T(1,128)} %reshape.110), calls=%async_computation.3 | async-start | bytes 131072 | tf_op jit(solution)/shard_map/all_to_all | solution.py:22
  124.8 0.8 multiply_multiply_fusion
  125.5 10.8 %all-to-all-done.3 = f32[16,1,1024]{2,1,0:T(1,128)S(1)} async-done(((f32[16,1,1024]{2,1,0:T(1,128)}), f32[16,1,1024]{2,1,0:T(1,128)S(1)}, u32[]{:S(2)}, u32[]{:S(2)}) %all-to-all-start.3) | async-done | bytes 65568 | tf_op jit(solution)/shard_map/all_to_all | solution.py:22
  136.3 0.8 reduce.9
  137.1 0.1 reshape.111
  137.2 0.0 copy-done.1
  137.3 0.0 copy-start
  137.3 0.2 select_reduce_fusion
  137.5 0.2 fusion.12
  137.6 0.3 convolution_add_fusion
  138.0 1.7 fusion.1
  139.7 5.7 %convolution_bitcast_fusion = f32[32,16,8,128]{3,2,1,0:T(8,128)S(1)} fusion(bf16[2048,256]{1,0:T(8,128)(2,1)S(1)} %fusion.1, bf16[2048,2048]{1,0:T(8,128)(2,1)} %all-gather.2.cloned.1.call-done), kind=kOutput, calls=%fused_computation.8 | convolution fusion | flops 2147483648 | bytes 11534336 | tf_op jit(solution)/shard_map/dot_general | solution.py:83
  145.5 0.0 copy-done
  145.5 0.2 copy.36
  145.7 31.3 %all_to_all.53 = f32[16,128,256]{1,2,0:T(8,128)S(1)} all-to-all(f32[16,128,256]{1,2,0:T(8,128)S(1)} %bitcast.31), channel_id=1, replica_groups=mesh['xl'=2,'y'=4,'c'=2,'z'=16,'xh'=2] {'xl','y','c'}, dimensions={0} | all-to-all | bytes 4194304 | tf_op jit(solution)/shard_map/all_to_all | solution.py:86
  177.0 1.8 copy.33
  (4 shorter events, 0.1 us)
Async XLA Ops:
  7.2 78.6 %all-gather.2.cloned.1.call-start = ((), (), s32[]{:S(2)}) async-start(), calls=%async_computation.5 | async-start | bytes 8912896 | tf_op jit(solution)/shard_map/all_gather | solution.py:40
  10.7 16.0 %all-to-all-start = ((s32[16,2,18]{2,1,0:T(2,128)}), s32[16,2,18]{2,1,0:T(2,128)S(1)}, u32[]{:S(2)}, u32[]{:S(2)}) async-start(s32[16,2,18]{2,1,0:T(2,128)} %broadcast_in_dim.12), calls=%async_computation | async-start | bytes 32768 | tf_op jit(solution)/shard_map/all_to_all | solution.py:22
  26.7 29.2 %all-to-all-start.1 = ((bf16[128,16,256]{0,2,1:T(8,128)(2,1)}), bf16[128,16,256]{0,2,1:T(8,128)(2,1)S(1)}, u32[]{:S(2)}, u32[]{:S(2)}) async-start(bf16[128,16,256]{0,2,1:T(8,128)(2,1)} %bitcast.3), calls=%async_computation.1 | async-start | bytes 2097152 | tf_op jit(solution)/shard_map/all_to_all | solution.py:39
  95.2 42.0 %copy-start.1 = (s32[32]{0:T(128)S(1)}, s32[32]{0:T(128)}, u32[]{:S(2)}) copy-start(s32[32]{0:T(128)} %param.11) | copy-start | bytes 388
  96.2 12.9 %all-to-all-start.2 = ((f32[32,1,1024]{2,1,0:T(1,128)}), f32[32,1,1024]{2,1,0:T(1,128)S(1)}, u32[]{:S(2)}, u32[]{:S(2)}) async-start(f32[32,1,1024]{2,1,0:T(1,128)} %reshape.108), calls=%async_computation.2 | async-start | bytes 262144 | tf_op jit(solution)/shard_map/all_to_all | solution.py:22
  111.6 24.7 %all-to-all-start.3 = ((f32[16,1,1024]{2,1,0:T(1,128)}), f32[16,1,1024]{2,1,0:T(1,128)S(1)}, u32[]{:S(2)}, u32[]{:S(2)}) async-start(f32[16,1,1024]{2,1,0:T(1,128)} %reshape.110), calls=%async_computation.3 | async-start | bytes 131072 | tf_op jit(solution)/shard_map/all_to_all | solution.py:22
  137.3 8.2 %copy-start = (f32[32,32]{1,0:T(8,128)}, f32[32,32]{1,0:T(8,128)S(1)}, u32[]{:S(2)}) copy-start(f32[32,32]{1,0:T(8,128)S(1)} %reduce_sum.75) | copy-start | bytes 12292
Sparse Core Ops, SparseCore 0:
  10.1 75.5 all-gather.1

commit v2 on v1

--- a/solution.py
+++ b/solution.py
@@ -3,10 +3,12 @@
 from jax import lax
 from jax.sharding import Mesh, PartitionSpec as P
 
+
 flops_weight = 0.3
 DP = ("xl", "y", "c")
 VOCAB = ("z", "xh")
 PLANE = ("xl", "y", "c", "xh")
+X = ("xl", "xh")
 
 
 def ranking_grad(scores, chosen, query_total):
@@ -24,6 +26,66 @@
     )
 
 
+def send_up(value, axis):
+    count = lax.axis_size(axis)
+    return lax.ppermute(value, axis, [(i, (i + 1) % count) for i in range(count)])
+
+
+def send_down(value, axis):
+    count = lax.axis_size(axis)
+    return lax.ppermute(value, axis, [((i + 1) % count, i) for i in range(count)])
+
+
+def x_slot(position):
+    return (position % 2) * 2 + position // 2
+
+
+def send_x_up(value):
+    return lax.ppermute(value, X, [(x_slot(i), x_slot((i + 1) % 4)) for i in range(4)])
+
+
+def send_x_down(value):
+    return lax.ppermute(value, X, [(x_slot((i + 1) % 4), x_slot(i)) for i in range(4)])
+
+
+def swap_x(value):
+    return lax.ppermute(value, X, [(x_slot(i), x_slot(i ^ 3)) for i in range(4)])
+
+
+def swap_cores(value):
+    return lax.ppermute(value, "c", [(0, 1), (1, 0)])
+
+
+STEPS = ((0, 0), (0, 3), (0, 1), (1, 0), (0, 2), (1, 3), (1, 1), (1, 2))
+
+
+def gather_hidden(own):
+    rows = own.shape[0] // 2
+    below = send_up(own, "y")
+    above = send_down(own, "y")
+    side = swap_x(own)
+    near = jnp.concatenate([own, below, above, side])
+    far_low = send_up(below[:rows], "y")
+    far_high = send_down(above[rows:], "y")
+    side_below = send_x_up(below)
+    side_above = send_x_down(above)
+    near_other = swap_cores(near)
+    corner_low = send_x_up(far_low)
+    corner_high = send_x_down(far_high)
+    rest = jnp.concatenate([far_low, far_high, side_below, side_above, corner_low, corner_high])
+    rest_other = swap_cores(rest)
+    return jnp.concatenate([near, rest, near_other, rest_other])
+
+
+def gathered_passages():
+    spot = jnp.arange(32, dtype=jnp.int32)
+    piece, half, other = spot // 2 % 8, spot % 2, spot // 16
+    flip = sum(jnp.where(piece == k, f, 0) for k, (f, _) in enumerate(STEPS))
+    step = sum(jnp.where(piece == k, s, 0) for k, (_, s) in enumerate(STEPS))
+    xl, y, c = lax.axis_index("xl"), lax.axis_index("y"), lax.axis_index("c")
+    return ((((xl + flip) & 1) * 4 + ((y + step) & 3)) * 2 + (c ^ other)) * 2 + half
+
+
 def local(passage_hidden, passage_lengths, query_ids, query_lengths, positives, head, df_prev):
     dp_count = lax.axis_size(DP)
     dp_index = lax.axis_index(DP)
@@ -35,10 +97,13 @@
     packed = spread(packed, DP).reshape(-1, query_slots + 2)
     query_tokens = packed[:, :query_slots]
     query_sizes = packed[:, query_slots]
-    passage_sizes = packed[:, query_slots + 1]
+    hidden_all = gather_hidden(passage_hidden)
+    passages = gathered_passages()
+    passage_count = packed.shape[0]
+    placed = passages[:, None] == jnp.arange(passage_count, dtype=jnp.int32)[None, :]
+    passage_sizes = jnp.sum(jnp.where(placed, packed[:, query_slots + 1][None, :], 0), axis=1)
+    placed = placed.astype(jnp.float32)
     head_block = lax.all_to_all(head, DP, split_axis=1, concat_axis=0, tiled=True)
-    hidden_all = lax.all_gather(passage_hidden, DP, axis=0, tiled=True)
-    passage_count = passage_sizes.shape[0]
     seq_span = hidden_all.shape[0] // passage_count
     logits = jnp.dot(hidden_all, head_block, preferred_element_type=jnp.float32)
     softened = jax.nn.softplus(logits)
@@ -67,12 +132,14 @@
         precision=lax.Precision.HIGHEST,
         preferred_element_type=jnp.float32,
     )
+    partial_scores = jnp.dot(partial_scores, placed, precision=lax.Precision.HIGHEST)
     query_total = positives.shape[0]
     plane_scores = jnp.sum(spread(partial_scores, PLANE), axis=0)
     scores = jnp.sum(spread(plane_scores, "z"), axis=0)
     score_grad = ranking_grad(scores, positives, query_total)
+    score_grad = jnp.dot(placed, score_grad.T, precision=lax.Precision.HIGHEST)
     rep_grad = jnp.dot(
-        score_grad.T, query_bag, precision=lax.Precision.HIGHEST, preferred_element_type=jnp.float32
+        score_grad, query_bag, precision=lax.Precision.HIGHEST, preferred_element_type=jnp.float32
     )
     rep_grad = rep_grad + 2.0 * flops_weight / passage_count * term_weight * jnp.mean(
         passage_rep, axis=0

time: 186 us -> 189 us (1.016)
  starting transfers between devices: 32.3 us -> 70.9 us
  waiting for transfers between devices: 76.5 us -> 38.6 us
  local copies, waits for them, and re-layouts: 9.72 us -> 23.5 us
  between operations: 14.2 us -> 1.02 us
    ppermute x0 -> x11, starting transfers between devices: none -> 42.5 us  [the longest x2 9.04 us: swap_cores(): return lax.ppermute(value, 'c', [(0, 1), (1, 0)])]
    all_gather x1 -> x0, waiting for transfers between devices: 29.3 us -> none  [local(): hidden_all = lax.all_gather(passage_hidden, DP, axis=0, tiled=True)]
    unnamed x10 -> x29, local copies, waits for them, and re-layouts: 6.06 us -> 15.7 us
    all_to_all x1, waiting for transfers between devices: 24.5 us -> 14.8 us  [local(): lax.all_to_all(head, DP, split_axis=1, concat_axis=0, tiled=True)]
    concatenate x0 -> x2, local copies, waits for them, and re-layouts: none -> 4.03 us  [the longest x1 3.18 us: gather_hidden(): return jnp.concatenate([near, rest, near_other, rest_other])]
    all_to_all x3, starting transfers between devices: 28.4 us -> 24.5 us  [spread(): lax.all_to_all(jnp.broadcast_to(value[None], (count,) + value.shape), axe...]
    ppermute x0 -> x11, waiting for transfers between devices: none -> 2.75 us  [the longest x2 2.66 us: send_x_up(): lax.ppermute(value, X, [(x_slot(i), x_slot((i + 1) % 4)) for i in range(4)])]
  transfers between devices with their start and end apart: 5 -> 15, of which waited for: 5 -> 6; matrix products, arithmetic and copies ran while one was open for 4% -> 11% of each run, Pallas kernels for 0% -> 0%
where the time goes in v2:
time: 189 us; the launch traced here: 188 us
  starting transfers between devices  70.9 us (38%)
  waiting for transfers between devices  38.6 us (20%)
  blocking collectives  31.3 us (17%)
  local copies, waits for them, and re-layouts  23.5 us (12%)
  matrix products  14.2 us (8%)
  other arithmetic  8.82 us (5%)
    all_to_all x1, blocking collectives, local(): lax.all_to_all(grad_block, DP, split_axis=0, concat_axis=1, tiled=True)  31.3 us
    all_to_all x3, starting transfers between devices, spread(): lax.all_to_all(jnp.broadcast_to(value[None], (count,) + value.shape), axe...  24.5 us
    all_to_all x3, waiting for transfers between devices, spread(): lax.all_to_all(jnp.broadcast_to(value[None], (count,) + value.shape), axe...  21 us
    unnamed x29, local copies, waits for them, and re-layouts  15.7 us
    all_to_all x1, waiting for transfers between devices, local(): lax.all_to_all(head, DP, split_axis=1, concat_axis=0, tiled=True)  14.8 us
    ppermute x2, starting transfers between devices, swap_cores(): return lax.ppermute(value, 'c', [(0, 1), (1, 0)])  9.04 us
    ppermute x2, starting transfers between devices, send_x_down(): lax.ppermute(value, X, [(x_slot((i + 1) % 4), x_slot(i)) for i in range(4)])  8.73 us
    ppermute x2, starting transfers between devices, send_up(): lax.ppermute(value, axis, [(i, (i + 1) % count) for i in range(count)])  8.61 us
  transfers between devices with their start and end apart: 15, of which 6 were waited for; matrix products, arithmetic and copies ran while one was open for 11% of the time, Pallas kernels for 0%

profile of v2, /device:TPU:1, one launch (start us, length us, event | category | flops | bytes accessed | tf_op | source)
XLA Modules:
  0.0 188.3 jit_solution(14814183807467183388)
XLA Ops:
  0.6 4.2 %collective-permute-start = (bf16[128,2048]{1,0:T(8,128)(2,1)}, bf16[128,2048]{1,0:T(8,128)(2,1)S(1)}, u32[]{:S(2)}, u32[]{:S(2)}) collective-permute-start(bf16[128,2048]{1,0:T(8,128)(2,1)} %param.7), channel_id=1, source_target_pairs={{0,64},{64,128},{128,192},{192,0},{1,65},{65,129},{129,193},{193,1... | collective-permute-start | bytes 1572872 | tf_op jit(solution)/shard_map/ppermute | solution.py:31
  4.8 3.4 %collective-permute-start.1 = (bf16[128,2048]{1,0:T(8,128)(2,1)}, bf16[128,2048]{1,0:T(8,128)(2,1)S(1)}, u32[]{:S(2)}, u32[]{:S(2)}) collective-permute-start(bf16[128,2048]{1,0:T(8,128)(2,1)} %param.7), channel_id=1, source_target_pairs={{64,0},{128,64},{192,128},{0,192},{65,1},{129,65},{193,129},{1,193... | collective-permute-start | bytes 1572872 | tf_op jit(solution)/shard_map/ppermute | solution.py:36
  8.2 4.4 %collective-permute-start.2 = (bf16[128,2048]{1,0:T(8,128)(2,1)}, bf16[128,2048]{1,0:T(8,128)(2,1)S(1)}, u32[]{:S(2)}, u32[]{:S(2)}) collective-permute-start(bf16[128,2048]{1,0:T(8,128)(2,1)} %param.7), channel_id=1, source_target_pairs={{0,257},{256,1},{1,256},{257,0},{2,259},{258,3},{3,258},{259,2},{4... | collective-permute-start | bytes 1572872 | tf_op jit(solution)/shard_map/ppermute | solution.py:52
  12.6 1.9 %constant_dynamic-update-slice_fusion.17 = bf16[2048,2048]{1,0:T(8,128)(2,1)} fusion(bf16[128,2048]{1,0:T(8,128)(2,1)} %param.7), kind=kLoop, calls=%fused_computation.27 | loop fusion | bytes 1048576
  14.5 4.5 %collective-permute-start.3 = (bf16[64,2048]{1,0:T(8,128)(2,1)S(1)}, bf16[64,2048]{1,0:T(8,128)(2,1)S(1)}, u32[]{:S(2)}, u32[]{:S(2)}) collective-permute-start(bf16[64,2048]{1,0:T(8,128)(2,1)S(1)} %slice.23), channel_id=1, source_target_pairs={{0,64},{64,128},{128,192},{192,0},{1,65},{65,129},{129,193},{193,1... | collective-permute-start | bytes 786440 | tf_op jit(solution)/shard_map/ppermute | solution.py:31
  19.0 4.2 %collective-permute-start.4 = (bf16[64,2048]{1,0:T(8,128)(2,1)S(1)}, bf16[64,2048]{1,0:T(8,128)(2,1)S(1)}, u32[]{:S(2)}, u32[]{:S(2)}) collective-permute-start(bf16[64,2048]{1,0:T(8,128)(2,1)S(1)} %slice.24), channel_id=1, source_target_pairs={{64,0},{128,64},{192,128},{0,192},{65,1},{129,65},{193,129},{1,193... | collective-permute-start | bytes 786440 | tf_op jit(solution)/shard_map/ppermute | solution.py:36
  23.2 1.5 pad_maximum_fusion
  24.7 6.0 %collective-permute-start.9 = (bf16[512,2048]{1,0:T(8,128)(2,1)}, bf16[512,2048]{1,0:T(8,128)(2,1)}, u32[]{:S(2)}, u32[]{:S(2)}) collective-permute-start(bf16[512,2048]{1,0:T(8,128)(2,1)} %pad_maximum_fusion), channel_id=1, source_target_pairs={{0,32},{32,0},{1,33},{33,1},{2,34},{34,2},{3,35},{35,3},{4,36},{36... | collective-permute-start | bytes 6291464 | tf_op jit(solution)/shard_map/ppermute | solution.py:56
  30.7 2.3 %collective-permute-start.5 = (bf16[128,2048]{1,0:T(8,128)(2,1)S(1)}, bf16[128,2048]{1,0:T(8,128)(2,1)S(1)}, u32[]{:S(2)}, u32[]{:S(2)}) collective-permute-start(bf16[128,2048]{1,0:T(8,128)(2,1)S(1)} %collective-permute-done), channel_id=1, source_target_pairs={{0,256},{256,1},{1,257},{257,0},{2,258},{258,3},{3,259},{259,2},{4... | collective-permute-start | bytes 1572872 | tf_op jit(solution)/shard_map/ppermute | solution.py:44
  33.0 4.2 %collective-permute-start.6 = (bf16[128,2048]{1,0:T(8,128)(2,1)S(1)}, bf16[128,2048]{1,0:T(8,128)(2,1)S(1)}, u32[]{:S(2)}, u32[]{:S(2)}) collective-permute-start(bf16[128,2048]{1,0:T(8,128)(2,1)S(1)} %collective-permute-done.1), channel_id=1, source_target_pairs={{256,0},{1,256},{257,1},{0,257},{258,2},{3,258},{259,3},{2,259},{2... | collective-permute-start | bytes 1572872 | tf_op jit(solution)/shard_map/ppermute | solution.py:48
  37.2 0.9 constant_dynamic-update-slice_fusion.16
  38.1 0.9 constant_dynamic-update-slice_fusion.15
  38.9 0.9 constant_dynamic-update-slice_fusion.14
  39.8 1.9 %collective-permute-start.7 = (bf16[64,2048]{1,0:T(8,128)(2,1)S(1)}, bf16[64,2048]{1,0:T(8,128)(2,1)S(1)}, u32[]{:S(2)}, u32[]{:S(2)}) collective-permute-start(bf16[64,2048]{1,0:T(8,128)(2,1)S(1)} %collective-permute-done.3), channel_id=1, source_target_pairs={{0,256},{256,1},{1,257},{257,0},{2,258},{258,3},{3,259},{259,2},{4... | collective-permute-start | bytes 786440 | tf_op jit(solution)/shard_map/ppermute | solution.py:44
  41.7 0.9 constant_dynamic-update-slice_fusion.5
  42.6 4.6 %collective-permute-start.8 = (bf16[64,2048]{1,0:T(8,128)(2,1)S(1)}, bf16[64,2048]{1,0:T(8,128)(2,1)S(1)}, u32[]{:S(2)}, u32[]{:S(2)}) collective-permute-start(bf16[64,2048]{1,0:T(8,128)(2,1)S(1)} %collective-permute-done.4), channel_id=1, source_target_pairs={{256,0},{1,256},{257,1},{0,257},{258,2},{3,258},{259,3},{2,259},{2... | collective-permute-start | bytes 786440 | tf_op jit(solution)/shard_map/ppermute | solution.py:48
  47.2 0.8 constant_dynamic-update-slice_fusion.4
  48.0 1.1 constant_dynamic-update-slice_fusion.3
  49.1 1.1 constant_dynamic-update-slice_fusion.2
  50.2 2.7 %collective-permute-done.7 = bf16[64,2048]{1,0:T(8,128)(2,1)S(1)} collective-permute-done((bf16[64,2048]{1,0:T(8,128)(2,1)S(1)}, bf16[64,2048]{1,0:T(8,128)(2,1)S(1)}, u32[]{:S(2)}, u32[]{:S(2)}) %collective-permute-start.7) | collective-permute-done | bytes 262176 | tf_op jit(solution)/shard_map/ppermute | solution.py:44
  52.9 0.8 constant_dynamic-update-slice_fusion.1
  53.8 0.8 constant_dynamic-update-slice_fusion
  54.6 3.0 %collective-permute-start.10 = (bf16[512,2048]{1,0:T(8,128)(2,1)}, bf16[512,2048]{1,0:T(8,128)(2,1)}, u32[]{:S(2)}, u32[]{:S(2)}) collective-permute-start(bf16[512,2048]{1,0:T(8,128)(2,1)} %get-tuple-element.8), channel_id=1, source_target_pairs={{0,32},{32,0},{1,33},{33,1},{2,34},{34,2},{3,35},{35,3},{4,36},{36... | collective-permute-start | bytes 6291464 | tf_op jit(solution)/shard_map/ppermute | solution.py:56
  58.0 0.6 broadcast_in_dim.91
  58.6 3.4 %all-to-all-start = ((s32[16,2,18]{2,1,0:T(2,128)}), s32[16,2,18]{2,1,0:T(2,128)S(1)}, u32[]{:S(2)}, u32[]{:S(2)}) async-start(s32[16,2,18]{2,1,0:T(2,128)} %broadcast_in_dim.91), calls=%async_computation | async-start | bytes 32768 | tf_op jit(solution)/shard_map/all_to_all | solution.py:24
  62.0 1.3 copy.24
  63.3 4.4 %all-to-all-done = s32[16,2,18]{2,1,0:T(2,128)S(1)} async-done(((s32[16,2,18]{2,1,0:T(2,128)}), s32[16,2,18]{2,1,0:T(2,128)S(1)}, u32[]{:S(2)}, u32[]{:S(2)}) %all-to-all-start) | async-done | bytes 2336 | tf_op jit(solution)/shard_map/all_to_all | solution.py:24
  67.8 3.8 %all-to-all-start.1 = ((bf16[128,16,256]{0,2,1:T(8,128)(2,1)}), bf16[128,16,256]{0,2,1:T(8,128)(2,1)S(1)}, u32[]{:S(2)}, u32[]{:S(2)}) async-start(bf16[128,16,256]{0,2,1:T(8,128)(2,1)} %bitcast.3), calls=%async_computation.1 | async-start | bytes 2097152 | tf_op jit(solution)/shard_map/all_to_all | solution.py:106
  72.5 14.8 %all-to-all-done.1 = bf16[128,16,256]{0,2,1:T(8,128)(2,1)S(1)} async-done(((bf16[128,16,256]{0,2,1:T(8,128)(2,1)}), bf16[128,16,256]{0,2,1:T(8,128)(2,1)S(1)}, u32[]{:S(2)}, u32[]{:S(2)}) %all-to-all-start.1) | async-done | bytes 1048608 | tf_op jit(solution)/shard_map/all_to_all | solution.py:106
  87.3 0.5 copy.25
  87.9 3.2 %constant_dynamic-update-slice_fusion.7 = bf16[2048,2048]{1,0:T(8,128)(2,1)} fusion(bf16[2048,2048]{1,0:T(8,128)(2,1)} %get-tuple-element.9, bf16[512,2048]{1,0:T(8,128)(2,1)} %collective-permute-done.9), kind=kLoop, calls=%fused_computation.17 | loop fusion | bytes 4194304
  91.1 3.2 %constant_dynamic-update-slice_fusion.6 = bf16[2048,2048]{1,0:T(8,128)(2,1)} fusion(bf16[2048,2048]{1,0:T(8,128)(2,1)} %constant_dynamic-update-slice_fusion.7, bf16[512,2048]{1,0:T(8,128)(2,1)} %collective-permute-done.10), kind=kLoop, calls=%fused_computation.16 | loop fusion | bytes 4194304 | tf_op jit(solution)/shard_map/concatenate | solution.py:77
  94.2 7.4 %multiply_reduce_fusion.1 = (f32[32,256]{1,0:T(8,128)S(1)}, f32[2048,256]{1,0:T(8,128)S(1)}) fusion(f32[32,64]{1,0:T(8,128)S(1)} %convert_divide_fusion, bf16[2048,2048]{1,0:T(8,128)(2,1)} %constant_dynamic-update-slice_fusion.6, bf16[2048,256]{1,0:T(8,128)(2,1)S(1)} %bitcast.30), kind=kOutput, calls=%fused_computation.6 | convolution fusion | flops 2151669760 | bytes 11575296 | tf_op jit(solution)/shard_map/dot_general | solution.py:108
  102.1 0.9 reshape.180
  103.0 6.3 %all-to-all-start.2 = ((f32[32,1,1024]{2,1,0:T(1,128)}), f32[32,1,1024]{2,1,0:T(1,128)S(1)}, u32[]{:S(2)}, u32[]{:S(2)}) async-start(f32[32,1,1024]{2,1,0:T(1,128)} %reshape.180), calls=%async_computation.2 | async-start | bytes 262144 | tf_op jit(solution)/shard_map/all_to_all | solution.py:24
  109.3 1.8 multiply_reduce_fusion
  111.2 5.8 %all-to-all-done.2 = f32[32,1,1024]{2,1,0:T(1,128)S(1)} async-done(((f32[32,1,1024]{2,1,0:T(1,128)}), f32[32,1,1024]{2,1,0:T(1,128)S(1)}, u32[]{:S(2)}, u32[]{:S(2)}) %all-to-all-start.2) | async-done | bytes 131104 | tf_op jit(solution)/shard_map/all_to_all | solution.py:24
  117.0 0.5 broadcast.347
  117.5 0.9 reduce.6
  118.7 0.8 reshape.182
  119.5 14.8 %all-to-all-start.3 = ((f32[16,1,1024]{2,1,0:T(1,128)}), f32[16,1,1024]{2,1,0:T(1,128)S(1)}, u32[]{:S(2)}, u32[]{:S(2)}) async-start(f32[16,1,1024]{2,1,0:T(1,128)} %reshape.182), calls=%async_computation.3 | async-start | bytes 131072 | tf_op jit(solution)/shard_map/all_to_all | solution.py:24
  134.4 0.8 multiply_multiply_fusion
  135.2 10.8 %all-to-all-done.3 = f32[16,1,1024]{2,1,0:T(1,128)S(1)} async-done(((f32[16,1,1024]{2,1,0:T(1,128)}), f32[16,1,1024]{2,1,0:T(1,128)S(1)}, u32[]{:S(2)}, u32[]{:S(2)}) %all-to-all-start.3) | async-done | bytes 65568 | tf_op jit(solution)/shard_map/all_to_all | solution.py:24
  145.9 0.8 reduce.7
  147.7 1.7 fusion.1
  149.4 6.0 %fusion.31 = f32[2048,256]{1,0:T(8,128)S(1)} fusion(bf16[2048,2048]{1,0:T(8,128)(2,1)} %constant_dynamic-update-slice_fusion.6, bf16[2048,256]{1,0:T(8,128)(2,1)S(1)} %fusion.1), kind=kOutput, calls=%fused_computation.90 | convolution fusion | flops 2147483648 | bytes 11534336 | tf_op jit(solution)/shard_map/dot_general | solution.py:150
  155.4 31.3 %all_to_all.53 = f32[16,128,256]{2,1,0:T(8,128)S(1)} all-to-all(f32[16,128,256]{2,1,0:T(8,128)S(1)} %bitcast.32), channel_id=1, replica_groups=mesh['xl'=2,'y'=4,'c'=2,'z'=16,'xh'=2] {'xl','y','c'}, dimensions={0} | all-to-all | bytes 4194304 | tf_op jit(solution)/shard_map/all_to_all | solution.py:153
  186.8 1.5 copy.27
  (51 shorter events, 2.9 us)
Async XLA Ops:
  0.6 22.5 %copy-start = (bf16[128,2048]{1,0:T(8,128)(2,1)S(1)}, bf16[128,2048]{1,0:T(8,128)(2,1)}, u32[]{:S(2)}) copy-start(bf16[128,2048]{1,0:T(8,128)(2,1)} %param.7) | copy-start | bytes 1572868
  0.6 13.8 %collective-permute-start = (bf16[128,2048]{1,0:T(8,128)(2,1)}, bf16[128,2048]{1,0:T(8,128)(2,1)S(1)}, u32[]{:S(2)}, u32[]{:S(2)}) collective-permute-start(bf16[128,2048]{1,0:T(8,128)(2,1)} %param.7), channel_id=1, source_target_pairs={{0,64},{64,128},{128,192},{192,0},{1,65},{65,129},{129,193},{193,1... | collective-permute-start | bytes 1572872 | tf_op jit(solution)/shard_map/ppermute | solution.py:31
  4.8 14.1 %collective-permute-start.1 = (bf16[128,2048]{1,0:T(8,128)(2,1)}, bf16[128,2048]{1,0:T(8,128)(2,1)S(1)}, u32[]{:S(2)}, u32[]{:S(2)}) collective-permute-start(bf16[128,2048]{1,0:T(8,128)(2,1)} %param.7), channel_id=1, source_target_pairs={{64,0},{128,64},{192,128},{0,192},{65,1},{129,65},{193,129},{1,193... | collective-permute-start | bytes 1572872 | tf_op jit(solution)/shard_map/ppermute | solution.py:36
  8.2 15.0 %collective-permute-start.2 = (bf16[128,2048]{1,0:T(8,128)(2,1)}, bf16[128,2048]{1,0:T(8,128)(2,1)S(1)}, u32[]{:S(2)}, u32[]{:S(2)}) collective-permute-start(bf16[128,2048]{1,0:T(8,128)(2,1)} %param.7), channel_id=1, source_target_pairs={{0,257},{256,1},{1,256},{257,0},{2,259},{258,3},{3,258},{259,2},{4... | collective-permute-start | bytes 1572872 | tf_op jit(solution)/shard_map/ppermute | solution.py:52
  14.5 25.3 %collective-permute-start.3 = (bf16[64,2048]{1,0:T(8,128)(2,1)S(1)}, bf16[64,2048]{1,0:T(8,128)(2,1)S(1)}, u32[]{:S(2)}, u32[]{:S(2)}) collective-permute-start(bf16[64,2048]{1,0:T(8,128)(2,1)S(1)} %slice.23), channel_id=1, source_target_pairs={{0,64},{64,128},{128,192},{192,0},{1,65},{65,129},{129,193},{193,1... | collective-permute-start | bytes 786440 | tf_op jit(solution)/shard_map/ppermute | solution.py:31
  19.0 23.6 %collective-permute-start.4 = (bf16[64,2048]{1,0:T(8,128)(2,1)S(1)}, bf16[64,2048]{1,0:T(8,128)(2,1)S(1)}, u32[]{:S(2)}, u32[]{:S(2)}) collective-permute-start(bf16[64,2048]{1,0:T(8,128)(2,1)S(1)} %slice.24), channel_id=1, source_target_pairs={{64,0},{128,64},{192,128},{0,192},{65,1},{129,65},{193,129},{1,193... | collective-permute-start | bytes 786440 | tf_op jit(solution)/shard_map/ppermute | solution.py:36
  24.7 63.2 %collective-permute-start.9 = (bf16[512,2048]{1,0:T(8,128)(2,1)}, bf16[512,2048]{1,0:T(8,128)(2,1)}, u32[]{:S(2)}, u32[]{:S(2)}) collective-permute-start(bf16[512,2048]{1,0:T(8,128)(2,1)} %pad_maximum_fusion), channel_id=1, source_target_pairs={{0,32},{32,0},{1,33},{33,1},{2,34},{34,2},{3,35},{35,3},{4,36},{36... | collective-permute-start | bytes 6291464 | tf_op jit(solution)/shard_map/ppermute | solution.py:56
  30.7 17.3 %collective-permute-start.5 = (bf16[128,2048]{1,0:T(8,128)(2,1)S(1)}, bf16[128,2048]{1,0:T(8,128)(2,1)S(1)}, u32[]{:S(2)}, u32[]{:S(2)}) collective-permute-start(bf16[128,2048]{1,0:T(8,128)(2,1)S(1)} %collective-permute-done), channel_id=1, source_target_pairs={{0,256},{256,1},{1,257},{257,0},{2,258},{258,3},{3,259},{259,2},{4... | collective-permute-start | bytes 1572872 | tf_op jit(solution)/shard_map/ppermute | solution.py:44
  33.0 16.1 %collective-permute-start.6 = (bf16[128,2048]{1,0:T(8,128)(2,1)S(1)}, bf16[128,2048]{1,0:T(8,128)(2,1)S(1)}, u32[]{:S(2)}, u32[]{:S(2)}) collective-permute-start(bf16[128,2048]{1,0:T(8,128)(2,1)S(1)} %collective-permute-done.1), channel_id=1, source_target_pairs={{256,0},{1,256},{257,1},{0,257},{258,2},{3,258},{259,3},{2,259},{2... | collective-permute-start | bytes 1572872 | tf_op jit(solution)/shard_map/ppermute | solution.py:48
  39.8 13.1 %collective-permute-start.7 = (bf16[64,2048]{1,0:T(8,128)(2,1)S(1)}, bf16[64,2048]{1,0:T(8,128)(2,1)S(1)}, u32[]{:S(2)}, u32[]{:S(2)}) collective-permute-start(bf16[64,2048]{1,0:T(8,128)(2,1)S(1)} %collective-permute-done.3), channel_id=1, source_target_pairs={{0,256},{256,1},{1,257},{257,0},{2,258},{258,3},{3,259},{259,2},{4... | collective-permute-start | bytes 786440 | tf_op jit(solution)/shard_map/ppermute | solution.py:44
  42.6 11.2 %collective-permute-start.8 = (bf16[64,2048]{1,0:T(8,128)(2,1)S(1)}, bf16[64,2048]{1,0:T(8,128)(2,1)S(1)}, u32[]{:S(2)}, u32[]{:S(2)}) collective-permute-start(bf16[64,2048]{1,0:T(8,128)(2,1)S(1)} %collective-permute-done.4), channel_id=1, source_target_pairs={{256,0},{1,256},{257,1},{0,257},{258,2},{3,258},{259,3},{2,259},{2... | collective-permute-start | bytes 786440 | tf_op jit(solution)/shard_map/ppermute | solution.py:48
  48.0 9.7 %copy-start.5 = (s32[2]{0:T(128)S(1)}, s32[2]{0:T(128)}, u32[]{:S(2)}) copy-start(s32[2]{0:T(128)} %param.10) | copy-start | bytes 28
  48.0 9.8 %copy-start.6 = (s32[2]{0:T(128)S(1)}, s32[2]{0:T(128)}, u32[]{:S(2)}) copy-start(s32[2]{0:T(128)} %param.8) | copy-start | bytes 28
  48.0 9.9 %copy-start.3 = (s32[2,16]{1,0:T(2,128)S(1)}, s32[2,16]{1,0:T(2,128)}, u32[]{:S(2)}) copy-start(s32[2,16]{1,0:T(2,128)} %param.9) | copy-start | bytes 388
  48.0 14.0 %copy-start.1 = (bf16[128,4096]{1,0:T(8,128)(2,1)S(1)}, bf16[128,4096]{1,0:T(8,128)(2,1)}, u32[]{:S(2)}) copy-start(bf16[128,4096]{1,0:T(8,128)(2,1)} %param.12) | copy-start | bytes 3145732
  54.6 36.4 %collective-permute-start.10 = (bf16[512,2048]{1,0:T(8,128)(2,1)}, bf16[512,2048]{1,0:T(8,128)(2,1)}, u32[]{:S(2)}, u32[]{:S(2)}) collective-permute-start(bf16[512,2048]{1,0:T(8,128)(2,1)} %get-tuple-element.8), channel_id=1, source_target_pairs={{0,32},{32,0},{1,33},{33,1},{2,34},{34,2},{3,35},{35,3},{4,36},{36... | collective-permute-start | bytes 6291464 | tf_op jit(solution)/shard_map/ppermute | solution.py:56
  58.6 9.2 %all-to-all-start = ((s32[16,2,18]{2,1,0:T(2,128)}), s32[16,2,18]{2,1,0:T(2,128)S(1)}, u32[]{:S(2)}, u32[]{:S(2)}) async-start(s32[16,2,18]{2,1,0:T(2,128)} %broadcast_in_dim.91), calls=%async_computation | async-start | bytes 32768 | tf_op jit(solution)/shard_map/all_to_all | solution.py:24
  67.8 19.6 %all-to-all-start.1 = ((bf16[128,16,256]{0,2,1:T(8,128)(2,1)}), bf16[128,16,256]{0,2,1:T(8,128)(2,1)S(1)}, u32[]{:S(2)}, u32[]{:S(2)}) async-start(bf16[128,16,256]{0,2,1:T(8,128)(2,1)} %bitcast.3), calls=%async_computation.1 | async-start | bytes 2097152 | tf_op jit(solution)/shard_map/all_to_all | solution.py:106
  103.0 14.0 %all-to-all-start.2 = ((f32[32,1,1024]{2,1,0:T(1,128)}), f32[32,1,1024]{2,1,0:T(1,128)S(1)}, u32[]{:S(2)}, u32[]{:S(2)}) async-start(f32[32,1,1024]{2,1,0:T(1,128)} %reshape.180), calls=%async_computation.2 | async-start | bytes 262144 | tf_op jit(solution)/shard_map/all_to_all | solution.py:24
  111.2 35.7 %copy-start.4 = (s32[32]{0:T(128)S(1)}, s32[32]{0:T(128)}, u32[]{:S(2)}) copy-start(s32[32]{0:T(128)} %param.11) | copy-start | bytes 388
  119.5 26.4 %all-to-all-start.3 = ((f32[16,1,1024]{2,1,0:T(1,128)}), f32[16,1,1024]{2,1,0:T(1,128)S(1)}, u32[]{:S(2)}, u32[]{:S(2)}) async-start(f32[16,1,1024]{2,1,0:T(1,128)} %reshape.182), calls=%async_computation.3 | async-start | bytes 131072 | tf_op jit(solution)/shard_map/all_to_all | solution.py:24
  146.9 8.5 %copy-start.2 = (f32[32,32]{1,0:T(8,128)}, f32[32,32]{1,0:T(8,128)S(1)}, u32[]{:S(2)}) copy-start(f32[32,32]{1,0:T(8,128)S(1)} %reduce_sum.85) | copy-start | bytes 12292

commit v3 on v2

--- a/solution.py
+++ b/solution.py
@@ -1,6 +1,7 @@
 import jax
 import jax.numpy as jnp
 from jax import lax
+from jax.experimental import pallas as pl
 from jax.sharding import Mesh, PartitionSpec as P
 
 
@@ -74,16 +75,46 @@
     corner_high = send_x_down(far_high)
     rest = jnp.concatenate([far_low, far_high, side_below, side_above, corner_low, corner_high])
     rest_other = swap_cores(rest)
-    return jnp.concatenate([near, rest, near_other, rest_other])
+    return near, near_other, rest, rest_other
 
 
 def gathered_passages():
     spot = jnp.arange(32, dtype=jnp.int32)
-    piece, half, other = spot // 2 % 8, spot % 2, spot // 16
+    piece, half, other = spot // 16 * 4 + spot // 2 % 4, spot % 2, spot // 8 % 2
     flip = sum(jnp.where(piece == k, f, 0) for k, (f, _) in enumerate(STEPS))
     step = sum(jnp.where(piece == k, s, 0) for k, (_, s) in enumerate(STEPS))
     xl, y, c = lax.axis_index("xl"), lax.axis_index("y"), lax.axis_index("c")
     return ((((xl + flip) & 1) * 4 + ((y + step) & 3)) * 2 + (c ^ other)) * 2 + half
+
+
+UNPACK = 4
+
+
+def unpack_rows(packet_ref, out_ref):
+    _, rows, columns = packet_ref.shape
+    for k in range(UNPACK):
+        packet = packet_ref[k]
+        unscale = jnp.exp2(-packet[rows - 8 : rows - 7])
+        out_ref[:, k * columns : (k + 1) * columns] = packet[: rows - 8] * unscale
+
+
+def return_rows(grad_block, dp_count):
+    depth, columns = grad_block.shape
+    peak = jnp.max(jnp.abs(grad_block))
+    power = jnp.clip(jnp.floor(14.0 - jnp.log2(peak)), -120.0, 120.0)
+    scaled = (grad_block * jnp.exp2(power)).reshape(dp_count, depth // dp_count, columns)
+    tag = jnp.full((dp_count, 8, columns), power)
+    packet = jnp.concatenate([scaled, tag], axis=1).astype(jnp.float16)
+    packet = lax.all_to_all(packet, DP, 0, 0, tiled=True).astype(jnp.float32)
+    rows = depth // dp_count
+    return pl.pallas_call(
+        unpack_rows,
+        grid=(dp_count // UNPACK,),
+        in_specs=[pl.BlockSpec((UNPACK, rows + 8, columns), lambda i: (i, 0, 0))],
+        out_specs=pl.BlockSpec((rows, UNPACK * columns), lambda i: (0, i)),
+        out_shape=jax.ShapeDtypeStruct((rows, dp_count * columns), jnp.float32),
+        name="unpack_rows",
+    )(packet)
 
 
 def local(passage_hidden, passage_lengths, query_ids, query_lengths, positives, head, df_prev):
@@ -97,23 +128,27 @@
     packed = spread(packed, DP).reshape(-1, query_slots + 2)
     query_tokens = packed[:, :query_slots]
     query_sizes = packed[:, query_slots]
-    hidden_all = gather_hidden(passage_hidden)
+    groups = gather_hidden(passage_hidden)
     passages = gathered_passages()
     passage_count = packed.shape[0]
     placed = passages[:, None] == jnp.arange(passage_count, dtype=jnp.int32)[None, :]
     passage_sizes = jnp.sum(jnp.where(placed, packed[:, query_slots + 1][None, :], 0), axis=1)
     placed = placed.astype(jnp.float32)
     head_block = lax.all_to_all(head, DP, split_axis=1, concat_axis=0, tiled=True)
-    seq_span = hidden_all.shape[0] // passage_count
-    logits = jnp.dot(hidden_all, head_block, preferred_element_type=jnp.float32)
-    softened = jax.nn.softplus(logits)
-    activation = jnp.log1p(softened)
-    slope_term = jax.nn.sigmoid(logits) / (1.0 + softened)
+    group_rows = groups[0].shape[0]
+    seq_span = group_rows * len(groups) // passage_count
+    logits = [jnp.dot(rows, head_block, preferred_element_type=jnp.float32) for rows in groups]
+    softened = [jax.nn.softplus(part) for part in logits]
+    slope_term = [jax.nn.sigmoid(part) / (1.0 + soft) for part, soft in zip(logits, softened)]
     positions = jnp.arange(seq_span, dtype=jnp.int32)
     token_mask = (positions[None, :] < passage_sizes[:, None]).astype(jnp.float32)
     token_weight = token_mask / passage_sizes.astype(jnp.float32)[:, None]
-    passage_rep = jnp.sum(
-        activation.reshape(passage_count, seq_span, column_count) * token_weight[:, :, None], axis=1
+    weight_of = jnp.split(token_weight, len(groups))
+    passage_rep = jnp.concatenate(
+        [
+            jnp.sum(jnp.log1p(soft).reshape(-1, seq_span, column_count) * weight[:, :, None], axis=1)
+            for soft, weight in zip(softened, weight_of)
+        ]
     )
     first_column = dp_index * column_count
     doc_freq = lax.dynamic_slice_in_dim(df_prev, first_column, column_count, 0) + jnp.sum(
@@ -144,14 +179,18 @@
     rep_grad = rep_grad + 2.0 * flops_weight / passage_count * term_weight * jnp.mean(
         passage_rep, axis=0
     )
-    logit_grad = (
-        (token_weight[:, :, None] * rep_grad[:, None, :]).reshape(logits.shape) * slope_term
-    ).astype(jnp.bfloat16)
-    grad_block = lax.dot_general(
-        hidden_all, logit_grad, (((0,), (0,)), ((), ())), preferred_element_type=jnp.float32
-    )
-    head_grad = lax.all_to_all(grad_block, DP, split_axis=0, concat_axis=1, tiled=True)
-    return (head_grad, scores)
+    grad_block = 0.0
+    for rows, weight, rep, slope in zip(
+        groups, weight_of, jnp.split(rep_grad, len(groups)), slope_term
+    ):
+        logit_grad = (weight[:, :, None] * rep[:, None, :]).reshape(slope.shape) * slope
+        grad_block += lax.dot_general(
+            rows,
+            logit_grad.astype(jnp.bfloat16),
+            (((0,), (0,)), ((), ())),
+            preferred_element_type=jnp.float32,
+        )
+    return (return_rows(grad_block, dp_count), scores)
 
 
 def solution(mesh):

time: 189 us -> 187 us (0.989)
  local copies, waits for them, and re-layouts: 23.5 us -> 13.8 us
  blocking collectives: 31.3 us -> 21.6 us
  matrix products: 14.2 us -> 21.4 us
  Pallas kernels: 0 us -> 3.83 us
  other arithmetic: 8.82 us -> 12.6 us
    all_to_all x1, blocking collectives: 31.3 us -> 21.6 us  [return_rows(): packet = lax.all_to_all(packet, DP, 0, 0, tiled=True).astype(jnp.float32)]
    dot_general x2 -> x8, matrix products: 13.4 us -> 20.7 us  [the longest x4 12.1 us: local(): jnp.dot(rows, head_block, preferred_element_type=jnp.float32)]
    ppermute x2, waiting for transfers between devices: 0.07 us -> 6.51 us  [send_x_down(): lax.ppermute(value, X, [(x_slot((i + 1) % 4), x_slot(i)) for i in range(4)])]
    unnamed x29 -> x33, local copies, waits for them, and re-layouts: 15.7 us -> 9.31 us
    pallas_call x0 -> x1, Pallas kernels: none -> 3.83 us  [return_rows(): pl.pallas_call(unpack_rows, grid=(dp_count // UNPACK,), in_specs=[pl.Bloc...]
    concatenate x1 -> x2, local copies, waits for them, and re-layouts: 3.18 us -> 0.31 us  [the longest x1 0.28 us: return_rows(): packet = jnp.concatenate([scaled, tag], axis=1).astype(jnp.float16)]
    ppermute x2, waiting for transfers between devices: 2.66 us -> 0.01 us  [send_x_up(): lax.ppermute(value, X, [(x_slot(i), x_slot((i + 1) % 4)) for i in range(4)])]
    convert_element_type x1 -> x5, other arithmetic: 1.73 us -> 4.32 us  [the longest x4 2.76 us: local(): logit_grad.astype(jnp.bfloat16)]
  transfers between devices with their start and end apart: 15 -> 15, of which waited for: 6 -> 6; matrix products, arithmetic and copies ran while one was open for 11% -> 13% of each run, Pallas kernels for 0% -> 0%
where the time goes in v3:
time: 187 us; the launch traced here: 186 us
  starting transfers between devices  71.2 us (38%)
  waiting for transfers between devices  39.6 us (21%)
  blocking collectives  21.6 us (12%)
  matrix products  21.4 us (11%)
  local copies, waits for them, and re-layouts  13.8 us (7%)
  other arithmetic  12.6 us (7%)
  Pallas kernels  3.83 us (2%)
  between operations  1.96 us (1%)
    all_to_all x3, starting transfers between devices, spread(): lax.all_to_all(jnp.broadcast_to(value[None], (count,) + value.shape), axe...  24.1 us
    all_to_all x1, blocking collectives, return_rows(): packet = lax.all_to_all(packet, DP, 0, 0, tiled=True).astype(jnp.float32)  21.6 us
    all_to_all x3, waiting for transfers between devices, spread(): lax.all_to_all(jnp.broadcast_to(value[None], (count,) + value.shape), axe...  18.4 us
    all_to_all x1, waiting for transfers between devices, local(): lax.all_to_all(head, DP, split_axis=1, concat_axis=0, tiled=True)  14.6 us
    dot_general x4, matrix products, local(): jnp.dot(rows, head_block, preferred_element_type=jnp.float32)  12.1 us
    unnamed x33, local copies, waits for them, and re-layouts  9.31 us
    ppermute x2, starting transfers between devices, send_up(): lax.ppermute(value, axis, [(i, (i + 1) % count) for i in range(count)])  9.25 us
    ppermute x2, starting transfers between devices, send_x_down(): lax.ppermute(value, X, [(x_slot((i + 1) % 4), x_slot(i)) for i in range(4)])  8.74 us
  transfers between devices with their start and end apart: 15, of which 6 were waited for; matrix products, arithmetic and copies ran while one was open for 13% of the time, Pallas kernels for 0%

profile of v3, /device:TPU:1, one launch (start us, length us, event | category | flops | bytes accessed | tf_op | source)
XLA Modules:
  0.0 186.0 jit_solution(5938895203908502360)
XLA Ops:
  0.6 4.0 %collective-permute-start = (bf16[128,2048]{1,0:T(8,128)(2,1)}, bf16[128,2048]{1,0:T(8,128)(2,1)S(1)}, u32[]{:S(2)}, u32[]{:S(2)}) collective-permute-start(bf16[128,2048]{1,0:T(8,128)(2,1)} %param.7), channel_id=1, source_target_pairs={{0,64},{64,128},{128,192},{192,0},{1,65},{65,129},{129,193},{193,1... | collective-permute-start | bytes 1572872 | tf_op jit(solution)/shard_map/ppermute | solution.py:32
  4.7 3.4 %collective-permute-start.1 = (bf16[128,2048]{1,0:T(8,128)(2,1)}, bf16[128,2048]{1,0:T(8,128)(2,1)S(1)}, u32[]{:S(2)}, u32[]{:S(2)}) collective-permute-start(bf16[128,2048]{1,0:T(8,128)(2,1)} %param.7), channel_id=1, source_target_pairs={{64,0},{128,64},{192,128},{0,192},{65,1},{129,65},{193,129},{1,193... | collective-permute-start | bytes 1572872 | tf_op jit(solution)/shard_map/ppermute | solution.py:37
  8.0 4.4 %collective-permute-start.2 = (bf16[128,2048]{1,0:T(8,128)(2,1)}, bf16[128,2048]{1,0:T(8,128)(2,1)S(1)}, u32[]{:S(2)}, u32[]{:S(2)}) collective-permute-start(bf16[128,2048]{1,0:T(8,128)(2,1)} %param.7), channel_id=1, source_target_pairs={{0,257},{256,1},{1,256},{257,0},{2,259},{258,3},{3,258},{259,2},{4... | collective-permute-start | bytes 1572872 | tf_op jit(solution)/shard_map/ppermute | solution.py:53
  12.4 1.1 constant_dynamic-update-slice_fusion.3
  13.6 5.2 %collective-permute-start.4 = (bf16[64,2048]{1,0:T(8,128)(2,1)S(1)}, bf16[64,2048]{1,0:T(8,128)(2,1)S(1)}, u32[]{:S(2)}, u32[]{:S(2)}) collective-permute-start(bf16[64,2048]{1,0:T(8,128)(2,1)S(1)} %slice.26), channel_id=1, source_target_pairs={{0,64},{64,128},{128,192},{192,0},{1,65},{65,129},{129,193},{193,1... | collective-permute-start | bytes 786440 | tf_op jit(solution)/shard_map/ppermute | solution.py:32
  18.8 4.2 %collective-permute-start.5 = (bf16[64,2048]{1,0:T(8,128)(2,1)S(1)}, bf16[64,2048]{1,0:T(8,128)(2,1)S(1)}, u32[]{:S(2)}, u32[]{:S(2)}) collective-permute-start(bf16[64,2048]{1,0:T(8,128)(2,1)S(1)} %slice.27), channel_id=1, source_target_pairs={{64,0},{128,64},{192,128},{0,192},{65,1},{129,65},{193,129},{1,193... | collective-permute-start | bytes 786440 | tf_op jit(solution)/shard_map/ppermute | solution.py:37
  23.0 4.4 %collective-permute-start.6 = (bf16[128,2048]{1,0:T(8,128)(2,1)S(1)}, bf16[128,2048]{1,0:T(8,128)(2,1)S(1)}, u32[]{:S(2)}, u32[]{:S(2)}) collective-permute-start(bf16[128,2048]{1,0:T(8,128)(2,1)S(1)} %collective-permute-done), channel_id=1, source_target_pairs={{0,256},{256,1},{1,257},{257,0},{2,258},{258,3},{3,259},{259,2},{4... | collective-permute-start | bytes 1572872 | tf_op jit(solution)/shard_map/ppermute | solution.py:45
  27.6 4.3 %collective-permute-start.3 = (bf16[512,2048]{1,0:T(8,128)(2,1)S(1)}, bf16[512,2048]{1,0:T(8,128)(2,1)}, u32[]{:S(2)}, u32[]{:S(2)}) collective-permute-start(bf16[512,2048]{1,0:T(8,128)(2,1)S(1)} %constant_dynamic-update-slice_fusion), channel_id=1, source_target_pairs={{0,32},{32,0},{1,33},{33,1},{2,34},{34,2},{3,35},{35,3},{4,36},{36... | collective-permute-start | bytes 6291464 | tf_op jit(solution)/shard_map/ppermute | solution.py:57
  31.9 4.2 %collective-permute-start.7 = (bf16[128,2048]{1,0:T(8,128)(2,1)S(1)}, bf16[128,2048]{1,0:T(8,128)(2,1)S(1)}, u32[]{:S(2)}, u32[]{:S(2)}) collective-permute-start(bf16[128,2048]{1,0:T(8,128)(2,1)S(1)} %collective-permute-done.1), channel_id=1, source_target_pairs={{256,0},{1,256},{257,1},{0,257},{258,2},{3,258},{259,3},{2,259},{2... | collective-permute-start | bytes 1572872 | tf_op jit(solution)/shard_map/ppermute | solution.py:49
  36.1 0.7 constant_dynamic-update-slice_fusion.9
  36.9 1.9 %collective-permute-start.8 = (bf16[64,2048]{1,0:T(8,128)(2,1)S(1)}, bf16[64,2048]{1,0:T(8,128)(2,1)S(1)}, u32[]{:S(2)}, u32[]{:S(2)}) collective-permute-start(bf16[64,2048]{1,0:T(8,128)(2,1)S(1)} %collective-permute-done.4), channel_id=1, source_target_pairs={{0,256},{256,1},{1,257},{257,0},{2,258},{258,3},{3,259},{259,2},{4... | collective-permute-start | bytes 786440 | tf_op jit(solution)/shard_map/ppermute | solution.py:45
  38.8 4.6 %collective-permute-start.9 = (bf16[64,2048]{1,0:T(8,128)(2,1)S(1)}, bf16[64,2048]{1,0:T(8,128)(2,1)S(1)}, u32[]{:S(2)}, u32[]{:S(2)}) collective-permute-start(bf16[64,2048]{1,0:T(8,128)(2,1)S(1)} %collective-permute-done.5), channel_id=1, source_target_pairs={{256,0},{1,256},{257,1},{0,257},{258,2},{3,258},{259,3},{2,259},{2... | collective-permute-start | bytes 786440 | tf_op jit(solution)/shard_map/ppermute | solution.py:49
  43.4 0.7 constant_dynamic-update-slice_fusion.8
  44.1 0.8 constant_dynamic-update-slice_fusion.7
  44.9 2.4 %collective-permute-done.7 = bf16[128,2048]{1,0:T(8,128)(2,1)S(1)} collective-permute-done((bf16[128,2048]{1,0:T(8,128)(2,1)S(1)}, bf16[128,2048]{1,0:T(8,128)(2,1)S(1)}, u32[]{:S(2)}, u32[]{:S(2)}) %collective-permute-start.7) | collective-permute-done | bytes 524320 | tf_op jit(solution)/shard_map/ppermute | solution.py:49
  47.4 0.8 constant_dynamic-update-slice_fusion.6
  48.9 4.1 %collective-permute-done.9 = bf16[64,2048]{1,0:T(8,128)(2,1)S(1)} collective-permute-done((bf16[64,2048]{1,0:T(8,128)(2,1)S(1)}, bf16[64,2048]{1,0:T(8,128)(2,1)S(1)}, u32[]{:S(2)}, u32[]{:S(2)}) %collective-permute-start.9) | collective-permute-done | bytes 262176 | tf_op jit(solution)/shard_map/ppermute | solution.py:49
  53.7 2.8 %collective-permute-start.10 = (bf16[512,2048]{1,0:T(8,128)(2,1)}, bf16[512,2048]{1,0:T(8,128)(2,1)}, u32[]{:S(2)}, u32[]{:S(2)}) collective-permute-start(bf16[512,2048]{1,0:T(8,128)(2,1)} %constant_dynamic-update-slice_fusion.4), channel_id=1, source_target_pairs={{0,32},{32,0},{1,33},{33,1},{2,34},{34,2},{3,35},{35,3},{4,36},{36... | collective-permute-start | bytes 6291464 | tf_op jit(solution)/shard_map/ppermute | solution.py:57
  57.4 3.4 %all-to-all-start = ((s32[16,2,18]{2,1,0:T(2,128)}), s32[16,2,18]{2,1,0:T(2,128)S(1)}, u32[]{:S(2)}, u32[]{:S(2)}) async-start(s32[16,2,18]{2,1,0:T(2,128)} %broadcast_in_dim.101), calls=%async_computation | async-start | bytes 32768 | tf_op jit(solution)/shard_map/all_to_all | solution.py:25
  60.8 1.3 copy.21
  62.2 4.4 %all-to-all-done = s32[16,2,18]{2,1,0:T(2,128)S(1)} async-done(((s32[16,2,18]{2,1,0:T(2,128)}), s32[16,2,18]{2,1,0:T(2,128)S(1)}, u32[]{:S(2)}, u32[]{:S(2)}) %all-to-all-start) | async-done | bytes 2336 | tf_op jit(solution)/shard_map/all_to_all | solution.py:25
  66.5 3.8 %all-to-all-start.1 = ((bf16[128,16,256]{0,2,1:T(8,128)(2,1)}), bf16[128,16,256]{0,2,1:T(8,128)(2,1)S(1)}, u32[]{:S(2)}, u32[]{:S(2)}) async-start(bf16[128,16,256]{0,2,1:T(8,128)(2,1)} %bitcast.3), calls=%async_computation.1 | async-start | bytes 2097152 | tf_op jit(solution)/shard_map/all_to_all | solution.py:137
  71.5 14.6 %all-to-all-done.1 = bf16[128,16,256]{0,2,1:T(8,128)(2,1)S(1)} async-done(((bf16[128,16,256]{0,2,1:T(8,128)(2,1)}), bf16[128,16,256]{0,2,1:T(8,128)(2,1)S(1)}, u32[]{:S(2)}, u32[]{:S(2)}) %all-to-all-start.1) | async-done | bytes 1048608 | tf_op jit(solution)/shard_map/all_to_all | solution.py:137
  86.1 1.0 copy-done
  87.1 1.5 copy.22
  88.6 1.8 multiply_reduce_fusion.7
  90.4 3.4 %multiply_reduce_fusion.5 = (f32[8,256]{1,0:T(8,128)S(1)}, f32[512,256]{1,0:T(8,128)}) fusion(f32[8,64]{1,0:T(8,128)S(1)} %get-tuple-element.10, bf16[512,2048]{1,0:T(8,128)(2,1)} %constant_dynamic-update-slice_fusion.4, bf16[2048,256]{1,0:T(8,128)(2,1)S(1)} %bitcast.61), kind=kOutput, calls=%fused_computation.28 | convolution fusion | flops 537917440 | bytes 3680256 | tf_op jit(solution)/shard_map/dot_general | solution.py:140
  93.8 3.4 %multiply_reduce_fusion.6 = (f32[8,256]{1,0:T(8,128)S(1)}, f32[512,256]{1,0:T(8,128)}) fusion(f32[8,64]{1,0:T(8,128)S(1)} %get-tuple-element.11, bf16[512,2048]{1,0:T(8,128)(2,1)} %collective-permute-done.3, bf16[2048,256]{1,0:T(8,128)(2,1)S(1)} %bitcast.62), kind=kOutput, calls=%fused_computation.30 | convolution fusion | flops 537917440 | bytes 3680256 | tf_op jit(solution)/shard_map/dot_general | solution.py:140
  97.3 3.4 %multiply_reduce_fusion.4 = (f32[8,256]{1,0:T(8,128)S(1)}, f32[512,256]{1,0:T(8,128)}) fusion(f32[8,64]{1,0:T(8,128)S(1)} %get-tuple-element.9, bf16[512,2048]{1,0:T(8,128)(2,1)} %collective-permute-done.10, bf16[2048,256]{1,0:T(8,128)(2,1)S(1)} %bitcast.63), kind=kOutput, calls=%fused_computation.26 | convolution fusion | flops 537917440 | bytes 3680256 | tf_op jit(solution)/shard_map/dot_general | solution.py:140
  101.1 0.9 reshape.193
  102.0 6.3 %all-to-all-start.2 = ((f32[32,1,1024]{2,1,0:T(1,128)}), f32[32,1,1024]{2,1,0:T(1,128)S(1)}, u32[]{:S(2)}, u32[]{:S(2)}) async-start(f32[32,1,1024]{2,1,0:T(1,128)} %reshape.193), calls=%async_computation.2 | async-start | bytes 262144 | tf_op jit(solution)/shard_map/all_to_all | solution.py:25
  108.3 2.1 %multiply_reduce_fusion.2 = (f32[256]{0:T(256)S(1)}, f32[256]{0:T(256)S(1)}) fusion(f32[512]{0:T(512)S(1)} %mul.232, f32[512,256]{1,0:T(8,128)} %get-tuple-element.17, f32[512]{0:T(512)S(1)} %mul.209, f32[512,256]{1,0:T(8,128)} %get-tuple-element.19), kind=kLoop, calls=%fused_computation.24 | loop fusion | flops 2096640 | bytes 1054720 | tf_op jit(solution)/shard_map/reduce_sum | solution.py:179
  110.4 5.5 %all-to-all-done.2 = f32[32,1,1024]{2,1,0:T(1,128)S(1)} async-done(((f32[32,1,1024]{2,1,0:T(1,128)}), f32[32,1,1024]{2,1,0:T(1,128)S(1)}, u32[]{:S(2)}, u32[]{:S(2)}) %all-to-all-start.2) | async-done | bytes 131104 | tf_op jit(solution)/shard_map/all_to_all | solution.py:25
  116.5 0.9 reduce.16
  117.7 0.8 reshape.195
  118.5 14.4 %all-to-all-start.3 = ((f32[16,1,1024]{2,1,0:T(1,128)}), f32[16,1,1024]{2,1,0:T(1,128)S(1)}, u32[]{:S(2)}, u32[]{:S(2)}) async-start(f32[16,1,1024]{2,1,0:T(1,128)} %reshape.195), calls=%async_computation.3 | async-start | bytes 131072 | tf_op jit(solution)/shard_map/all_to_all | solution.py:25
  132.9 2.2 %multiply_reduce_fusion = (f32[256]{0:T(256)S(1)}, f32[256]{0:T(256)S(1)}) fusion(f32[512]{0:T(512)S(1)} %mul.238, f32[512,256]{1,0:T(8,128)} %get-tuple-element.13, f32[512]{0:T(512)S(1)} %mul.235, f32[512,256]{1,0:T(8,128)} %get-tuple-element.15), kind=kLoop, calls=%fused_computation.22 | loop fusion | flops 2096640 | bytes 1054720 | tf_op jit(solution)/shard_map/reduce_sum | solution.py:179
  135.2 0.8 multiply_multiply_fusion
  135.9 8.6 %all-to-all-done.3 = f32[16,1,1024]{2,1,0:T(1,128)S(1)} async-done(((f32[16,1,1024]{2,1,0:T(1,128)}), f32[16,1,1024]{2,1,0:T(1,128)S(1)}, u32[]{:S(2)}, u32[]{:S(2)}) %all-to-all-start.3) | async-done | bytes 65568 | tf_op jit(solution)/shard_map/all_to_all | solution.py:25
  144.5 0.8 reduce.17
  146.3 1.5 fusion.4
  149.1 2.3 %fusion.48 = f32[2048,256]{1,0:T(8,128)S(1)} fusion(bf16[512,2048]{1,0:T(8,128)(2,1)} %collective-permute-done.3, bf16[512,256]{1,0:T(8,128)(2,1)S(1)} %fusion.6), kind=kOutput, calls=%fused_computation.121 | convolution fusion | flops 536870912 | bytes 4456448 | tf_op jit(solution)/shard_map/dot_general | solution.py:187
  151.4 0.8 convolution_add_fusion.1
  152.2 2.3 %fusion.49 = f32[2048,256]{1,0:T(8,128)S(1)} fusion(bf16[512,2048]{1,0:T(8,128)(2,1)} %collective-permute-done.10, bf16[512,256]{1,0:T(8,128)(2,1)S(1)} %fusion.2), kind=kOutput, calls=%fused_computation.122 | convolution fusion | flops 536870912 | bytes 4456448 | tf_op jit(solution)/shard_map/dot_general | solution.py:187
  154.5 3.1 %abs_reduce_fusion = (f32[]{:T(128)}, f32[2048,256]{1,0:T(8,128)S(1)}) fusion(f32[2048,256]{1,0:T(8,128)S(1)} %fusion.49, f32[2048,256]{1,0:T(8,128)S(1)} %convolution_add_fusion.1, bf16[512,2048]{1,0:T(8,128)(2,1)} %constant_dynamic-update-slice_fusion.4, bf16[512,256]{1,0:T(8,128)(2,1)S(1)} %fusion.4), kind=kOutput, calls=%fused_computation.4 | convolution fusion | flops 538968064 | bytes 8650756 | tf_op jit(solution)/shard_map/dot_general | solution.py:187
  159.0 21.6 %all_to_all.39 = f16[16,136,256]{2,1,0:T(8,128)(2,1)S(1)} all-to-all(f16[16,136,256]{2,1,0:T(8,128)(2,1)S(1)} %concatenate.19), channel_id=1, replica_groups=mesh['xl'=2,'y'=4,'c'=2,'z'=16,'xh'=2] {'xl','y','c'}, dimensions={0} | all-to-all | bytes 2228224 | tf_op jit(solution)/shard_map/all_to_all | solution.py:108
  180.6 1.6 convert_element_type.38.packet_ref
  182.2 3.8 %unpack_rows.1 = f32[128,4096]{1,0:T(8,128)} custom-call(f32[16,136,256]{2,1,0:T(8,128)} %convert_element_type.38.packet_ref), custom_call_target="tpu_custom_call" | custom-call | tf_op jit(solution)/shard_map/unpack_rows/pallas_call | solution.py:110
  (72 shorter events, 7.6 us)
Async XLA Ops:
  0.6 12.9 %collective-permute-start = (bf16[128,2048]{1,0:T(8,128)(2,1)}, bf16[128,2048]{1,0:T(8,128)(2,1)S(1)}, u32[]{:S(2)}, u32[]{:S(2)}) collective-permute-start(bf16[128,2048]{1,0:T(8,128)(2,1)} %param.7), channel_id=1, source_target_pairs={{0,64},{64,128},{128,192},{192,0},{1,65},{65,129},{129,193},{193,1... | collective-permute-start | bytes 1572872 | tf_op jit(solution)/shard_map/ppermute | solution.py:32
  4.7 14.1 %collective-permute-start.1 = (bf16[128,2048]{1,0:T(8,128)(2,1)}, bf16[128,2048]{1,0:T(8,128)(2,1)S(1)}, u32[]{:S(2)}, u32[]{:S(2)}) collective-permute-start(bf16[128,2048]{1,0:T(8,128)(2,1)} %param.7), channel_id=1, source_target_pairs={{64,0},{128,64},{192,128},{0,192},{65,1},{129,65},{193,129},{1,193... | collective-permute-start | bytes 1572872 | tf_op jit(solution)/shard_map/ppermute | solution.py:37
  8.0 19.5 %collective-permute-start.2 = (bf16[128,2048]{1,0:T(8,128)(2,1)}, bf16[128,2048]{1,0:T(8,128)(2,1)S(1)}, u32[]{:S(2)}, u32[]{:S(2)}) collective-permute-start(bf16[128,2048]{1,0:T(8,128)(2,1)} %param.7), channel_id=1, source_target_pairs={{0,257},{256,1},{1,256},{257,0},{2,259},{258,3},{3,258},{259,2},{4... | collective-permute-start | bytes 1572872 | tf_op jit(solution)/shard_map/ppermute | solution.py:53
  13.6 22.6 %collective-permute-start.4 = (bf16[64,2048]{1,0:T(8,128)(2,1)S(1)}, bf16[64,2048]{1,0:T(8,128)(2,1)S(1)}, u32[]{:S(2)}, u32[]{:S(2)}) collective-permute-start(bf16[64,2048]{1,0:T(8,128)(2,1)S(1)} %slice.26), channel_id=1, source_target_pairs={{0,64},{64,128},{128,192},{192,0},{1,65},{65,129},{129,193},{193,1... | collective-permute-start | bytes 786440 | tf_op jit(solution)/shard_map/ppermute | solution.py:32
  18.8 19.9 %collective-permute-start.5 = (bf16[64,2048]{1,0:T(8,128)(2,1)S(1)}, bf16[64,2048]{1,0:T(8,128)(2,1)S(1)}, u32[]{:S(2)}, u32[]{:S(2)}) collective-permute-start(bf16[64,2048]{1,0:T(8,128)(2,1)S(1)} %slice.27), channel_id=1, source_target_pairs={{64,0},{128,64},{192,128},{0,192},{65,1},{129,65},{193,129},{1,193... | collective-permute-start | bytes 786440 | tf_op jit(solution)/shard_map/ppermute | solution.py:37
  23.0 21.1 %collective-permute-start.6 = (bf16[128,2048]{1,0:T(8,128)(2,1)S(1)}, bf16[128,2048]{1,0:T(8,128)(2,1)S(1)}, u32[]{:S(2)}, u32[]{:S(2)}) collective-permute-start(bf16[128,2048]{1,0:T(8,128)(2,1)S(1)} %collective-permute-done), channel_id=1, source_target_pairs={{0,256},{256,1},{1,257},{257,0},{2,258},{258,3},{3,259},{259,2},{4... | collective-permute-start | bytes 1572872 | tf_op jit(solution)/shard_map/ppermute | solution.py:45
  27.5 28.9 %copy-start.8 = (s32[2]{0:T(128)S(1)}, s32[2]{0:T(128)}, u32[]{:S(2)}) copy-start(s32[2]{0:T(128)} %param.10) | copy-start | bytes 28
  27.6 29.0 %copy-start.9 = (s32[2]{0:T(128)S(1)}, s32[2]{0:T(128)}, u32[]{:S(2)}) copy-start(s32[2]{0:T(128)} %param.8) | copy-start | bytes 28
  27.6 29.1 %copy-start.6 = (s32[2,16]{1,0:T(2,128)S(1)}, s32[2,16]{1,0:T(2,128)}, u32[]{:S(2)}) copy-start(s32[2,16]{1,0:T(2,128)} %param.9) | copy-start | bytes 388
  27.6 33.3 %copy-start.4 = (bf16[128,4096]{1,0:T(8,128)(2,1)S(1)}, bf16[128,4096]{1,0:T(8,128)(2,1)}, u32[]{:S(2)}) copy-start(bf16[128,4096]{1,0:T(8,128)(2,1)} %param.12) | copy-start | bytes 3145732
  27.6 66.2 %collective-permute-start.3 = (bf16[512,2048]{1,0:T(8,128)(2,1)S(1)}, bf16[512,2048]{1,0:T(8,128)(2,1)}, u32[]{:S(2)}, u32[]{:S(2)}) collective-permute-start(bf16[512,2048]{1,0:T(8,128)(2,1)S(1)} %constant_dynamic-update-slice_fusion), channel_id=1, source_target_pairs={{0,32},{32,0},{1,33},{33,1},{2,34},{34,2},{3,35},{35,3},{4,36},{36... | collective-permute-start | bytes 6291464 | tf_op jit(solution)/shard_map/ppermute | solution.py:57
  31.9 15.4 %collective-permute-start.7 = (bf16[128,2048]{1,0:T(8,128)(2,1)S(1)}, bf16[128,2048]{1,0:T(8,128)(2,1)S(1)}, u32[]{:S(2)}, u32[]{:S(2)}) collective-permute-start(bf16[128,2048]{1,0:T(8,128)(2,1)S(1)} %collective-permute-done.1), channel_id=1, source_target_pairs={{256,0},{1,256},{257,1},{0,257},{258,2},{3,258},{259,3},{2,259},{2... | collective-permute-start | bytes 1572872 | tf_op jit(solution)/shard_map/ppermute | solution.py:49
  36.9 11.3 %collective-permute-start.8 = (bf16[64,2048]{1,0:T(8,128)(2,1)S(1)}, bf16[64,2048]{1,0:T(8,128)(2,1)S(1)}, u32[]{:S(2)}, u32[]{:S(2)}) collective-permute-start(bf16[64,2048]{1,0:T(8,128)(2,1)S(1)} %collective-permute-done.4), channel_id=1, source_target_pairs={{0,256},{256,1},{1,257},{257,0},{2,258},{258,3},{3,259},{259,2},{4... | collective-permute-start | bytes 786440 | tf_op jit(solution)/shard_map/ppermute | solution.py:45
  38.8 14.2 %collective-permute-start.9 = (bf16[64,2048]{1,0:T(8,128)(2,1)S(1)}, bf16[64,2048]{1,0:T(8,128)(2,1)S(1)}, u32[]{:S(2)}, u32[]{:S(2)}) collective-permute-start(bf16[64,2048]{1,0:T(8,128)(2,1)S(1)} %collective-permute-done.5), channel_id=1, source_target_pairs={{256,0},{1,256},{257,1},{0,257},{258,2},{3,258},{259,3},{2,259},{2... | collective-permute-start | bytes 786440 | tf_op jit(solution)/shard_map/ppermute | solution.py:49
  53.7 43.6 %collective-permute-start.10 = (bf16[512,2048]{1,0:T(8,128)(2,1)}, bf16[512,2048]{1,0:T(8,128)(2,1)}, u32[]{:S(2)}, u32[]{:S(2)}) collective-permute-start(bf16[512,2048]{1,0:T(8,128)(2,1)} %constant_dynamic-update-slice_fusion.4), channel_id=1, source_target_pairs={{0,32},{32,0},{1,33},{33,1},{2,34},{34,2},{3,35},{35,3},{4,36},{36... | collective-permute-start | bytes 6291464 | tf_op jit(solution)/shard_map/ppermute | solution.py:57
  57.4 9.2 %all-to-all-start = ((s32[16,2,18]{2,1,0:T(2,128)}), s32[16,2,18]{2,1,0:T(2,128)S(1)}, u32[]{:S(2)}, u32[]{:S(2)}) async-start(s32[16,2,18]{2,1,0:T(2,128)} %broadcast_in_dim.101), calls=%async_computation | async-start | bytes 32768 | tf_op jit(solution)/shard_map/all_to_all | solution.py:25
  66.5 19.6 %all-to-all-start.1 = ((bf16[128,16,256]{0,2,1:T(8,128)(2,1)}), bf16[128,16,256]{0,2,1:T(8,128)(2,1)S(1)}, u32[]{:S(2)}, u32[]{:S(2)}) async-start(bf16[128,16,256]{0,2,1:T(8,128)(2,1)} %bitcast.3), calls=%async_computation.1 | async-start | bytes 2097152 | tf_op jit(solution)/shard_map/all_to_all | solution.py:137
  86.1 1.0 copy-start
  102.0 14.0 %all-to-all-start.2 = ((f32[32,1,1024]{2,1,0:T(1,128)}), f32[32,1,1024]{2,1,0:T(1,128)S(1)}, u32[]{:S(2)}, u32[]{:S(2)}) async-start(f32[32,1,1024]{2,1,0:T(1,128)} %reshape.193), calls=%async_computation.2 | async-start | bytes 262144 | tf_op jit(solution)/shard_map/all_to_all | solution.py:25
  117.4 28.0 %copy-start.7 = (s32[32]{0:T(128)S(1)}, s32[32]{0:T(128)}, u32[]{:S(2)}) copy-start(s32[32]{0:T(128)} %param.11) | copy-start | bytes 388
  117.7 30.1 %copy-start.1 = (f32[512,256]{1,0:T(8,128)S(1)}, f32[512,256]{1,0:T(8,128)}, u32[]{:S(2)}) copy-start(f32[512,256]{1,0:T(8,128)} %get-tuple-element.19) | copy-start | bytes 1572868
  118.5 26.0 %all-to-all-start.3 = ((f32[16,1,1024]{2,1,0:T(1,128)}), f32[16,1,1024]{2,1,0:T(1,128)S(1)}, u32[]{:S(2)}, u32[]{:S(2)}) async-start(f32[16,1,1024]{2,1,0:T(1,128)} %reshape.195), calls=%async_computation.3 | async-start | bytes 131072 | tf_op jit(solution)/shard_map/all_to_all | solution.py:25
  132.9 15.3 %copy-start.2 = (f32[512,256]{1,0:T(8,128)S(1)}, f32[512,256]{1,0:T(8,128)}, u32[]{:S(2)}) copy-start(f32[512,256]{1,0:T(8,128)} %get-tuple-element.17) | copy-start | bytes 1572868
  145.4 6.0 %copy-start.5 = (f32[32,32]{1,0:T(8,128)}, f32[32,32]{1,0:T(8,128)S(1)}, u32[]{:S(2)}) copy-start(f32[32,32]{1,0:T(8,128)S(1)} %reduce_sum.139) | copy-start | bytes 12292
  145.5 3.2 %copy-start.3 = (f32[512,256]{1,0:T(8,128)S(1)}, f32[512,256]{1,0:T(8,128)}, u32[]{:S(2)}) copy-start(f32[512,256]{1,0:T(8,128)} %get-tuple-element.13) | copy-start | bytes 1572868

commit v4 on v2

--- a/solution.py
+++ b/solution.py
@@ -1,6 +1,7 @@
 import jax
 import jax.numpy as jnp
 from jax import lax
+from jax.experimental.layout import Layout, with_layout_constraint
 from jax.sharding import Mesh, PartitionSpec as P
 
 
@@ -86,6 +87,21 @@
     return ((((xl + flip) & 1) * 4 + ((y + step) & 3)) * 2 + (c ^ other)) * 2 + half
 
 
+def return_rows(grad_block, dp_count):
+    depth, columns = grad_block.shape
+    peak = jnp.max(jnp.abs(grad_block))
+    power = jnp.clip(jnp.floor(14.0 - jnp.log2(peak)), -120.0, 120.0)
+    scaled = (grad_block * jnp.exp2(power)).reshape(dp_count, depth // dp_count, columns)
+    tag = jnp.full((dp_count, 8, columns), power)
+    packet = jnp.concatenate([scaled, tag], axis=1).astype(jnp.float16)
+    packet = lax.all_to_all(packet, DP, 0, 0, tiled=True).astype(jnp.float32)
+    packet = with_layout_constraint(packet, Layout((0, 1, 2)))
+    rows = packet[:, :-8] * jnp.exp2(-packet[:, -1:, :1])
+    bands = rows.reshape(dp_count, -1, 8, columns).transpose(1, 0, 2, 3)
+    bands = lax.optimization_barrier(with_layout_constraint(bands, Layout((0, 1, 2, 3))))
+    return bands.transpose(0, 2, 1, 3).reshape(depth // dp_count, dp_count * columns)
+
+
 def local(passage_hidden, passage_lengths, query_ids, query_lengths, positives, head, df_prev):
     dp_count = lax.axis_size(DP)
     dp_index = lax.axis_index(DP)
@@ -150,8 +166,7 @@
     grad_block = lax.dot_general(
         hidden_all, logit_grad, (((0,), (0,)), ((), ())), preferred_element_type=jnp.float32
     )
-    head_grad = lax.all_to_all(grad_block, DP, split_axis=0, concat_axis=1, tiled=True)
-    return (head_grad, scores)
+    return (return_rows(grad_block, dp_count), scores)
 
 
 def solution(mesh):

time: 189 us -> 182 us (0.963)
  blocking collectives: 31.3 us -> 21.6 us
  other arithmetic: 8.82 us -> 11.1 us
    all_to_all x1, blocking collectives: 31.3 us -> 21.6 us  [return_rows(): packet = lax.all_to_all(packet, DP, 0, 0, tiled=True).astype(jnp.float32)]
  transfers between devices with their start and end apart: 15 -> 15, of which waited for: 6 -> 6; matrix products, arithmetic and copies ran while one was open for 11% -> 12% of each run, Pallas kernels for 0% -> 0%
where the time goes in v4:
time: 182 us; the launch traced here: 181 us
  starting transfers between devices  70.9 us (39%)
  waiting for transfers between devices  38.6 us (21%)
  local copies, waits for them, and re-layouts  22.3 us (12%)
  blocking collectives  21.6 us (12%)
  matrix products  14.7 us (8%)
  other arithmetic  11.1 us (6%)
    all_to_all x3, starting transfers between devices, spread(): lax.all_to_all(jnp.broadcast_to(value[None], (count,) + value.shape), axe...  24.5 us
    all_to_all x1, blocking collectives, return_rows(): packet = lax.all_to_all(packet, DP, 0, 0, tiled=True).astype(jnp.float32)  21.6 us
    all_to_all x3, waiting for transfers between devices, spread(): lax.all_to_all(jnp.broadcast_to(value[None], (count,) + value.shape), axe...  21 us
    unnamed x29, local copies, waits for them, and re-layouts  15.7 us
    all_to_all x1, waiting for transfers between devices, local(): lax.all_to_all(head, DP, split_axis=1, concat_axis=0, tiled=True)  14.8 us
    ppermute x2, starting transfers between devices, swap_cores(): return lax.ppermute(value, 'c', [(0, 1), (1, 0)])  9.04 us
    ppermute x2, starting transfers between devices, send_x_down(): lax.ppermute(value, X, [(x_slot((i + 1) % 4), x_slot(i)) for i in range(4)])  8.73 us
    ppermute x2, starting transfers between devices, send_up(): lax.ppermute(value, axis, [(i, (i + 1) % count) for i in range(count)])  8.61 us
  transfers between devices with their start and end apart: 15, of which 6 were waited for; matrix products, arithmetic and copies ran while one was open for 12% of the time, Pallas kernels for 0%

profile of v4, /device:TPU:1, one launch (start us, length us, event | category | flops | bytes accessed | tf_op | source)
XLA Modules:
  0.0 180.8 jit_solution(15147251518178669134)
XLA Ops:
  0.6 4.2 %collective-permute-start = (bf16[128,2048]{1,0:T(8,128)(2,1)}, bf16[128,2048]{1,0:T(8,128)(2,1)S(1)}, u32[]{:S(2)}, u32[]{:S(2)}) collective-permute-start(bf16[128,2048]{1,0:T(8,128)(2,1)} %param.7), channel_id=1, source_target_pairs={{0,64},{64,128},{128,192},{192,0},{1,65},{65,129},{129,193},{193,1... | collective-permute-start | bytes 1572872 | tf_op jit(solution)/shard_map/ppermute | solution.py:32
  4.8 3.4 %collective-permute-start.1 = (bf16[128,2048]{1,0:T(8,128)(2,1)}, bf16[128,2048]{1,0:T(8,128)(2,1)S(1)}, u32[]{:S(2)}, u32[]{:S(2)}) collective-permute-start(bf16[128,2048]{1,0:T(8,128)(2,1)} %param.7), channel_id=1, source_target_pairs={{64,0},{128,64},{192,128},{0,192},{65,1},{129,65},{193,129},{1,193... | collective-permute-start | bytes 1572872 | tf_op jit(solution)/shard_map/ppermute | solution.py:37
  8.2 4.4 %collective-permute-start.2 = (bf16[128,2048]{1,0:T(8,128)(2,1)}, bf16[128,2048]{1,0:T(8,128)(2,1)S(1)}, u32[]{:S(2)}, u32[]{:S(2)}) collective-permute-start(bf16[128,2048]{1,0:T(8,128)(2,1)} %param.7), channel_id=1, source_target_pairs={{0,257},{256,1},{1,256},{257,0},{2,259},{258,3},{3,258},{259,2},{4... | collective-permute-start | bytes 1572872 | tf_op jit(solution)/shard_map/ppermute | solution.py:53
  12.6 1.9 %constant_dynamic-update-slice_fusion.17 = bf16[2048,2048]{1,0:T(8,128)(2,1)} fusion(bf16[128,2048]{1,0:T(8,128)(2,1)} %param.7), kind=kLoop, calls=%fused_computation.32 | loop fusion | bytes 1048576
  14.5 4.5 %collective-permute-start.3 = (bf16[64,2048]{1,0:T(8,128)(2,1)S(1)}, bf16[64,2048]{1,0:T(8,128)(2,1)S(1)}, u32[]{:S(2)}, u32[]{:S(2)}) collective-permute-start(bf16[64,2048]{1,0:T(8,128)(2,1)S(1)} %slice.31), channel_id=1, source_target_pairs={{0,64},{64,128},{128,192},{192,0},{1,65},{65,129},{129,193},{193,1... | collective-permute-start | bytes 786440 | tf_op jit(solution)/shard_map/ppermute | solution.py:32
  19.0 4.2 %collective-permute-start.4 = (bf16[64,2048]{1,0:T(8,128)(2,1)S(1)}, bf16[64,2048]{1,0:T(8,128)(2,1)S(1)}, u32[]{:S(2)}, u32[]{:S(2)}) collective-permute-start(bf16[64,2048]{1,0:T(8,128)(2,1)S(1)} %slice.32), channel_id=1, source_target_pairs={{64,0},{128,64},{192,128},{0,192},{65,1},{129,65},{193,129},{1,193... | collective-permute-start | bytes 786440 | tf_op jit(solution)/shard_map/ppermute | solution.py:37
  23.2 1.5 pad_maximum_fusion
  24.7 6.0 %collective-permute-start.9 = (bf16[512,2048]{1,0:T(8,128)(2,1)}, bf16[512,2048]{1,0:T(8,128)(2,1)}, u32[]{:S(2)}, u32[]{:S(2)}) collective-permute-start(bf16[512,2048]{1,0:T(8,128)(2,1)} %pad_maximum_fusion), channel_id=1, source_target_pairs={{0,32},{32,0},{1,33},{33,1},{2,34},{34,2},{3,35},{35,3},{4,36},{36... | collective-permute-start | bytes 6291464 | tf_op jit(solution)/shard_map/ppermute | solution.py:57
  30.7 2.3 %collective-permute-start.5 = (bf16[128,2048]{1,0:T(8,128)(2,1)S(1)}, bf16[128,2048]{1,0:T(8,128)(2,1)S(1)}, u32[]{:S(2)}, u32[]{:S(2)}) collective-permute-start(bf16[128,2048]{1,0:T(8,128)(2,1)S(1)} %collective-permute-done), channel_id=1, source_target_pairs={{0,256},{256,1},{1,257},{257,0},{2,258},{258,3},{3,259},{259,2},{4... | collective-permute-start | bytes 1572872 | tf_op jit(solution)/shard_map/ppermute | solution.py:45
  33.0 4.2 %collective-permute-start.6 = (bf16[128,2048]{1,0:T(8,128)(2,1)S(1)}, bf16[128,2048]{1,0:T(8,128)(2,1)S(1)}, u32[]{:S(2)}, u32[]{:S(2)}) collective-permute-start(bf16[128,2048]{1,0:T(8,128)(2,1)S(1)} %collective-permute-done.1), channel_id=1, source_target_pairs={{256,0},{1,256},{257,1},{0,257},{258,2},{3,258},{259,3},{2,259},{2... | collective-permute-start | bytes 1572872 | tf_op jit(solution)/shard_map/ppermute | solution.py:49
  37.2 0.9 constant_dynamic-update-slice_fusion.16
  38.1 0.9 constant_dynamic-update-slice_fusion.15
  38.9 0.9 constant_dynamic-update-slice_fusion.14
  39.8 1.9 %collective-permute-start.7 = (bf16[64,2048]{1,0:T(8,128)(2,1)S(1)}, bf16[64,2048]{1,0:T(8,128)(2,1)S(1)}, u32[]{:S(2)}, u32[]{:S(2)}) collective-permute-start(bf16[64,2048]{1,0:T(8,128)(2,1)S(1)} %collective-permute-done.3), channel_id=1, source_target_pairs={{0,256},{256,1},{1,257},{257,0},{2,258},{258,3},{3,259},{259,2},{4... | collective-permute-start | bytes 786440 | tf_op jit(solution)/shard_map/ppermute | solution.py:45
  41.7 0.9 constant_dynamic-update-slice_fusion.5
  42.6 4.6 %collective-permute-start.8 = (bf16[64,2048]{1,0:T(8,128)(2,1)S(1)}, bf16[64,2048]{1,0:T(8,128)(2,1)S(1)}, u32[]{:S(2)}, u32[]{:S(2)}) collective-permute-start(bf16[64,2048]{1,0:T(8,128)(2,1)S(1)} %collective-permute-done.4), channel_id=1, source_target_pairs={{256,0},{1,256},{257,1},{0,257},{258,2},{3,258},{259,3},{2,259},{2... | collective-permute-start | bytes 786440 | tf_op jit(solution)/shard_map/ppermute | solution.py:49
  47.2 0.8 constant_dynamic-update-slice_fusion.4
  48.0 1.1 constant_dynamic-update-slice_fusion.3
  49.1 1.1 constant_dynamic-update-slice_fusion.2
  50.2 2.7 %collective-permute-done.7 = bf16[64,2048]{1,0:T(8,128)(2,1)S(1)} collective-permute-done((bf16[64,2048]{1,0:T(8,128)(2,1)S(1)}, bf16[64,2048]{1,0:T(8,128)(2,1)S(1)}, u32[]{:S(2)}, u32[]{:S(2)}) %collective-permute-start.7) | collective-permute-done | bytes 262176 | tf_op jit(solution)/shard_map/ppermute | solution.py:45
  52.9 0.8 constant_dynamic-update-slice_fusion.1
  53.8 0.8 constant_dynamic-update-slice_fusion
  54.6 3.0 %collective-permute-start.10 = (bf16[512,2048]{1,0:T(8,128)(2,1)}, bf16[512,2048]{1,0:T(8,128)(2,1)}, u32[]{:S(2)}, u32[]{:S(2)}) collective-permute-start(bf16[512,2048]{1,0:T(8,128)(2,1)} %get-tuple-element.8), channel_id=1, source_target_pairs={{0,32},{32,0},{1,33},{33,1},{2,34},{34,2},{3,35},{35,3},{4,36},{36... | collective-permute-start | bytes 6291464 | tf_op jit(solution)/shard_map/ppermute | solution.py:57
  58.0 0.6 broadcast_in_dim.92
  58.6 3.4 %all-to-all-start = ((s32[16,2,18]{2,1,0:T(2,128)}), s32[16,2,18]{2,1,0:T(2,128)S(1)}, u32[]{:S(2)}, u32[]{:S(2)}) async-start(s32[16,2,18]{2,1,0:T(2,128)} %broadcast_in_dim.92), calls=%async_computation | async-start | bytes 32768 | tf_op jit(solution)/shard_map/all_to_all | solution.py:25
  62.0 1.3 copy.23
  63.3 4.4 %all-to-all-done = s32[16,2,18]{2,1,0:T(2,128)S(1)} async-done(((s32[16,2,18]{2,1,0:T(2,128)}), s32[16,2,18]{2,1,0:T(2,128)S(1)}, u32[]{:S(2)}, u32[]{:S(2)}) %all-to-all-start) | async-done | bytes 2336 | tf_op jit(solution)/shard_map/all_to_all | solution.py:25
  67.8 3.8 %all-to-all-start.1 = ((bf16[128,16,256]{0,2,1:T(8,128)(2,1)}), bf16[128,16,256]{0,2,1:T(8,128)(2,1)S(1)}, u32[]{:S(2)}, u32[]{:S(2)}) async-start(bf16[128,16,256]{0,2,1:T(8,128)(2,1)} %bitcast.3), calls=%async_computation.1 | async-start | bytes 2097152 | tf_op jit(solution)/shard_map/all_to_all | solution.py:122
  72.5 14.8 %all-to-all-done.1 = bf16[128,16,256]{0,2,1:T(8,128)(2,1)S(1)} async-done(((bf16[128,16,256]{0,2,1:T(8,128)(2,1)}), bf16[128,16,256]{0,2,1:T(8,128)(2,1)S(1)}, u32[]{:S(2)}, u32[]{:S(2)}) %all-to-all-start.1) | async-done | bytes 1048608 | tf_op jit(solution)/shard_map/all_to_all | solution.py:122
  87.3 0.5 copy.24
  87.9 3.2 %constant_dynamic-update-slice_fusion.7 = bf16[2048,2048]{1,0:T(8,128)(2,1)} fusion(bf16[2048,2048]{1,0:T(8,128)(2,1)} %get-tuple-element.9, bf16[512,2048]{1,0:T(8,128)(2,1)} %collective-permute-done.9), kind=kLoop, calls=%fused_computation.22 | loop fusion | bytes 4194304
  91.1 3.2 %constant_dynamic-update-slice_fusion.6 = bf16[2048,2048]{1,0:T(8,128)(2,1)} fusion(bf16[2048,2048]{1,0:T(8,128)(2,1)} %constant_dynamic-update-slice_fusion.7, bf16[512,2048]{1,0:T(8,128)(2,1)} %collective-permute-done.10), kind=kLoop, calls=%fused_computation.21 | loop fusion | bytes 4194304 | tf_op jit(solution)/shard_map/concatenate | solution.py:78
  94.2 7.4 %multiply_reduce_fusion.1 = (f32[32,256]{1,0:T(8,128)S(1)}, f32[2048,256]{1,0:T(8,128)S(1)}) fusion(f32[32,64]{1,0:T(8,128)S(1)} %convert_divide_fusion, bf16[2048,2048]{1,0:T(8,128)(2,1)} %constant_dynamic-update-slice_fusion.6, bf16[2048,256]{1,0:T(8,128)(2,1)S(1)} %bitcast.35), kind=kOutput, calls=%fused_computation.11 | convolution fusion | flops 2151669760 | bytes 11575296 | tf_op jit(solution)/shard_map/dot_general | solution.py:124
  102.1 0.9 reshape.191
  103.0 6.3 %all-to-all-start.2 = ((f32[32,1,1024]{2,1,0:T(1,128)}), f32[32,1,1024]{2,1,0:T(1,128)S(1)}, u32[]{:S(2)}, u32[]{:S(2)}) async-start(f32[32,1,1024]{2,1,0:T(1,128)} %reshape.191), calls=%async_computation.2 | async-start | bytes 262144 | tf_op jit(solution)/shard_map/all_to_all | solution.py:25
  109.3 1.8 %multiply_reduce_fusion = f32[256]{0:T(256)S(1)} fusion(f32[2048]{0:T(1024)S(1)} %div.51, f32[2048,256]{1,0:T(8,128)S(1)} %get-tuple-element.17), kind=kLoop, calls=%fused_computation.10 | loop fusion | flops 4194048 | bytes 2106368 | tf_op jit(solution)/shard_map/reduce_sum | solution.py:160
  111.2 5.8 %all-to-all-done.2 = f32[32,1,1024]{2,1,0:T(1,128)S(1)} async-done(((f32[32,1,1024]{2,1,0:T(1,128)}), f32[32,1,1024]{2,1,0:T(1,128)S(1)}, u32[]{:S(2)}, u32[]{:S(2)}) %all-to-all-start.2) | async-done | bytes 131104 | tf_op jit(solution)/shard_map/all_to_all | solution.py:25
  117.0 0.5 broadcast.355
  117.5 0.9 reduce.8
  118.7 0.8 reshape.193
  119.5 14.8 %all-to-all-start.3 = ((f32[16,1,1024]{2,1,0:T(1,128)}), f32[16,1,1024]{2,1,0:T(1,128)S(1)}, u32[]{:S(2)}, u32[]{:S(2)}) async-start(f32[16,1,1024]{2,1,0:T(1,128)} %reshape.193), calls=%async_computation.3 | async-start | bytes 131072 | tf_op jit(solution)/shard_map/all_to_all | solution.py:25
  134.4 0.8 multiply_multiply_fusion
  135.2 10.8 %all-to-all-done.3 = f32[16,1,1024]{2,1,0:T(1,128)S(1)} async-done(((f32[16,1,1024]{2,1,0:T(1,128)}), f32[16,1,1024]{2,1,0:T(1,128)S(1)}, u32[]{:S(2)}, u32[]{:S(2)}) %all-to-all-start.3) | async-done | bytes 65568 | tf_op jit(solution)/shard_map/all_to_all | solution.py:25
  145.9 0.8 reduce.9
  147.7 1.7 fusion.2
  149.4 6.5 %abs_reduce_fusion = (f32[]{:T(128)}, f32[2048,256]{1,0:T(8,128)S(1)}) fusion(bf16[2048,2048]{1,0:T(8,128)(2,1)} %constant_dynamic-update-slice_fusion.6, bf16[2048,256]{1,0:T(8,128)(2,1)S(1)} %fusion.2), kind=kOutput, calls=%fused_computation.9 | convolution fusion | flops 2148532224 | bytes 11534340 | tf_op jit(solution)/shard_map/dot_general | solution.py:166
  157.2 21.6 %all_to_all.39 = f16[16,136,256]{2,1,0:T(8,128)(2,1)S(1)} all-to-all(f16[16,136,256]{2,1,0:T(8,128)(2,1)S(1)} %concatenate.20), channel_id=1, replica_groups=mesh['xl'=2,'y'=4,'c'=2,'z'=16,'xh'=2] {'xl','y','c'}, dimensions={0} | all-to-all | bytes 2228224 | tf_op jit(solution)/shard_map/all_to_all | solution.py:97
  179.2 1.6 copy_bitcast_fusion
  (55 shorter events, 3.8 us)
Async XLA Ops:
  0.6 22.5 %copy-start = (bf16[128,2048]{1,0:T(8,128)(2,1)S(1)}, bf16[128,2048]{1,0:T(8,128)(2,1)}, u32[]{:S(2)}) copy-start(bf16[128,2048]{1,0:T(8,128)(2,1)} %param.7) | copy-start | bytes 1572868
  0.6 13.8 %collective-permute-start = (bf16[128,2048]{1,0:T(8,128)(2,1)}, bf16[128,2048]{1,0:T(8,128)(2,1)S(1)}, u32[]{:S(2)}, u32[]{:S(2)}) collective-permute-start(bf16[128,2048]{1,0:T(8,128)(2,1)} %param.7), channel_id=1, source_target_pairs={{0,64},{64,128},{128,192},{192,0},{1,65},{65,129},{129,193},{193,1... | collective-permute-start | bytes 1572872 | tf_op jit(solution)/shard_map/ppermute | solution.py:32
  4.8 14.1 %collective-permute-start.1 = (bf16[128,2048]{1,0:T(8,128)(2,1)}, bf16[128,2048]{1,0:T(8,128)(2,1)S(1)}, u32[]{:S(2)}, u32[]{:S(2)}) collective-permute-start(bf16[128,2048]{1,0:T(8,128)(2,1)} %param.7), channel_id=1, source_target_pairs={{64,0},{128,64},{192,128},{0,192},{65,1},{129,65},{193,129},{1,193... | collective-permute-start | bytes 1572872 | tf_op jit(solution)/shard_map/ppermute | solution.py:37
  8.2 15.0 %collective-permute-start.2 = (bf16[128,2048]{1,0:T(8,128)(2,1)}, bf16[128,2048]{1,0:T(8,128)(2,1)S(1)}, u32[]{:S(2)}, u32[]{:S(2)}) collective-permute-start(bf16[128,2048]{1,0:T(8,128)(2,1)} %param.7), channel_id=1, source_target_pairs={{0,257},{256,1},{1,256},{257,0},{2,259},{258,3},{3,258},{259,2},{4... | collective-permute-start | bytes 1572872 | tf_op jit(solution)/shard_map/ppermute | solution.py:53
  14.5 25.3 %collective-permute-start.3 = (bf16[64,2048]{1,0:T(8,128)(2,1)S(1)}, bf16[64,2048]{1,0:T(8,128)(2,1)S(1)}, u32[]{:S(2)}, u32[]{:S(2)}) collective-permute-start(bf16[64,2048]{1,0:T(8,128)(2,1)S(1)} %slice.31), channel_id=1, source_target_pairs={{0,64},{64,128},{128,192},{192,0},{1,65},{65,129},{129,193},{193,1... | collective-permute-start | bytes 786440 | tf_op jit(solution)/shard_map/ppermute | solution.py:32
  19.0 23.6 %collective-permute-start.4 = (bf16[64,2048]{1,0:T(8,128)(2,1)S(1)}, bf16[64,2048]{1,0:T(8,128)(2,1)S(1)}, u32[]{:S(2)}, u32[]{:S(2)}) collective-permute-start(bf16[64,2048]{1,0:T(8,128)(2,1)S(1)} %slice.32), channel_id=1, source_target_pairs={{64,0},{128,64},{192,128},{0,192},{65,1},{129,65},{193,129},{1,193... | collective-permute-start | bytes 786440 | tf_op jit(solution)/shard_map/ppermute | solution.py:37
  24.7 63.2 %collective-permute-start.9 = (bf16[512,2048]{1,0:T(8,128)(2,1)}, bf16[512,2048]{1,0:T(8,128)(2,1)}, u32[]{:S(2)}, u32[]{:S(2)}) collective-permute-start(bf16[512,2048]{1,0:T(8,128)(2,1)} %pad_maximum_fusion), channel_id=1, source_target_pairs={{0,32},{32,0},{1,33},{33,1},{2,34},{34,2},{3,35},{35,3},{4,36},{36... | collective-permute-start | bytes 6291464 | tf_op jit(solution)/shard_map/ppermute | solution.py:57
  30.7 17.3 %collective-permute-start.5 = (bf16[128,2048]{1,0:T(8,128)(2,1)S(1)}, bf16[128,2048]{1,0:T(8,128)(2,1)S(1)}, u32[]{:S(2)}, u32[]{:S(2)}) collective-permute-start(bf16[128,2048]{1,0:T(8,128)(2,1)S(1)} %collective-permute-done), channel_id=1, source_target_pairs={{0,256},{256,1},{1,257},{257,0},{2,258},{258,3},{3,259},{259,2},{4... | collective-permute-start | bytes 1572872 | tf_op jit(solution)/shard_map/ppermute | solution.py:45
  33.0 16.1 %collective-permute-start.6 = (bf16[128,2048]{1,0:T(8,128)(2,1)S(1)}, bf16[128,2048]{1,0:T(8,128)(2,1)S(1)}, u32[]{:S(2)}, u32[]{:S(2)}) collective-permute-start(bf16[128,2048]{1,0:T(8,128)(2,1)S(1)} %collective-permute-done.1), channel_id=1, source_target_pairs={{256,0},{1,256},{257,1},{0,257},{258,2},{3,258},{259,3},{2,259},{2... | collective-permute-start | bytes 1572872 | tf_op jit(solution)/shard_map/ppermute | solution.py:49
  39.8 13.1 %collective-permute-start.7 = (bf16[64,2048]{1,0:T(8,128)(2,1)S(1)}, bf16[64,2048]{1,0:T(8,128)(2,1)S(1)}, u32[]{:S(2)}, u32[]{:S(2)}) collective-permute-start(bf16[64,2048]{1,0:T(8,128)(2,1)S(1)} %collective-permute-done.3), channel_id=1, source_target_pairs={{0,256},{256,1},{1,257},{257,0},{2,258},{258,3},{3,259},{259,2},{4... | collective-permute-start | bytes 786440 | tf_op jit(solution)/shard_map/ppermute | solution.py:45
  42.6 11.2 %collective-permute-start.8 = (bf16[64,2048]{1,0:T(8,128)(2,1)S(1)}, bf16[64,2048]{1,0:T(8,128)(2,1)S(1)}, u32[]{:S(2)}, u32[]{:S(2)}) collective-permute-start(bf16[64,2048]{1,0:T(8,128)(2,1)S(1)} %collective-permute-done.4), channel_id=1, source_target_pairs={{256,0},{1,256},{257,1},{0,257},{258,2},{3,258},{259,3},{2,259},{2... | collective-permute-start | bytes 786440 | tf_op jit(solution)/shard_map/ppermute | solution.py:49
  48.0 9.7 %copy-start.5 = (s32[2]{0:T(128)S(1)}, s32[2]{0:T(128)}, u32[]{:S(2)}) copy-start(s32[2]{0:T(128)} %param.10) | copy-start | bytes 28
  48.0 9.8 %copy-start.6 = (s32[2]{0:T(128)S(1)}, s32[2]{0:T(128)}, u32[]{:S(2)}) copy-start(s32[2]{0:T(128)} %param.8) | copy-start | bytes 28
  48.0 9.9 %copy-start.3 = (s32[2,16]{1,0:T(2,128)S(1)}, s32[2,16]{1,0:T(2,128)}, u32[]{:S(2)}) copy-start(s32[2,16]{1,0:T(2,128)} %param.9) | copy-start | bytes 388
  48.0 14.0 %copy-start.1 = (bf16[128,4096]{1,0:T(8,128)(2,1)S(1)}, bf16[128,4096]{1,0:T(8,128)(2,1)}, u32[]{:S(2)}) copy-start(bf16[128,4096]{1,0:T(8,128)(2,1)} %param.12) | copy-start | bytes 3145732
  54.6 36.4 %collective-permute-start.10 = (bf16[512,2048]{1,0:T(8,128)(2,1)}, bf16[512,2048]{1,0:T(8,128)(2,1)}, u32[]{:S(2)}, u32[]{:S(2)}) collective-permute-start(bf16[512,2048]{1,0:T(8,128)(2,1)} %get-tuple-element.8), channel_id=1, source_target_pairs={{0,32},{32,0},{1,33},{33,1},{2,34},{34,2},{3,35},{35,3},{4,36},{36... | collective-permute-start | bytes 6291464 | tf_op jit(solution)/shard_map/ppermute | solution.py:57
  58.6 9.2 %all-to-all-start = ((s32[16,2,18]{2,1,0:T(2,128)}), s32[16,2,18]{2,1,0:T(2,128)S(1)}, u32[]{:S(2)}, u32[]{:S(2)}) async-start(s32[16,2,18]{2,1,0:T(2,128)} %broadcast_in_dim.92), calls=%async_computation | async-start | bytes 32768 | tf_op jit(solution)/shard_map/all_to_all | solution.py:25
  67.8 19.6 %all-to-all-start.1 = ((bf16[128,16,256]{0,2,1:T(8,128)(2,1)}), bf16[128,16,256]{0,2,1:T(8,128)(2,1)S(1)}, u32[]{:S(2)}, u32[]{:S(2)}) async-start(bf16[128,16,256]{0,2,1:T(8,128)(2,1)} %bitcast.3), calls=%async_computation.1 | async-start | bytes 2097152 | tf_op jit(solution)/shard_map/all_to_all | solution.py:122
  103.0 14.0 %all-to-all-start.2 = ((f32[32,1,1024]{2,1,0:T(1,128)}), f32[32,1,1024]{2,1,0:T(1,128)S(1)}, u32[]{:S(2)}, u32[]{:S(2)}) async-start(f32[32,1,1024]{2,1,0:T(1,128)} %reshape.191), calls=%async_computation.2 | async-start | bytes 262144 | tf_op jit(solution)/shard_map/all_to_all | solution.py:25
  111.2 35.7 %copy-start.4 = (s32[32]{0:T(128)S(1)}, s32[32]{0:T(128)}, u32[]{:S(2)}) copy-start(s32[32]{0:T(128)} %param.11) | copy-start | bytes 388
  119.5 26.4 %all-to-all-start.3 = ((f32[16,1,1024]{2,1,0:T(1,128)}), f32[16,1,1024]{2,1,0:T(1,128)S(1)}, u32[]{:S(2)}, u32[]{:S(2)}) async-start(f32[16,1,1024]{2,1,0:T(1,128)} %reshape.193), calls=%async_computation.3 | async-start | bytes 131072 | tf_op jit(solution)/shard_map/all_to_all | solution.py:25
  146.9 9.0 %copy-start.2 = (f32[32,32]{1,0:T(8,128)}, f32[32,32]{1,0:T(8,128)S(1)}, u32[]{:S(2)}) copy-start(f32[32,32]{1,0:T(8,128)S(1)} %reduce_sum.85) | copy-start | bytes 12292
